TPU v7x, 256 devices: a whole 4x4x8 slice. The times are simulated.
256 devices in a mesh: seq: 32 (over x, y, core), head: 8 (over z).
Axes of the slice: x: 4, y: 4, z: 8, core: 2. Of those that a mesh axis runs over, the one named last changes fastest.
Arguments:
- queries: bfloat16 [12288, 3072], P('seq', 'head'), may hold values from -8 to 8
- key_states: bfloat16 [12288, 3072], P('seq', 'head'), may hold values from -8 to 8
- value_states: bfloat16 [12288, 3072], P('seq', 'head'), may hold values from -6 to 6
- block_lists: int32 [96, 4], replicated, may hold values from 0 to 95, as said below
- out_weight: bfloat16 [3072, 3072], P('head'), may hold values from -0.15625 to 0.15625
- out_grad: bfloat16 [12288, 3072], P('seq', 'head'), may hold values from -6 to 6
Outputs:
- attended: bfloat16 [12288, 3072], P('seq', 'head')
- query_grad: bfloat16 [12288, 3072], P('seq', 'head')
- key_grad: bfloat16 [12288, 3072], P('seq', 'head')
- value_grad: bfloat16 [12288, 3072], P('seq', 'head')
Inputs may be any that keep to these rules, and one draw needn't show every extreme that they name: `block_lists`: row r names 4 different blocks, among them block r itself; 2 of them lie in r's own group of 3 blocks and 2 in other groups. Of each group's blocks at most two are named by rows of other groups, and the rows of one group name at most one block of any other group.
All inputs are finite; a program needn't handle non-finite values.
Results may differ from a plain program's by a relative error of at most 0.035.
Values may be sent and summed in bfloat16 or wider, within the bound.
No kernel may reach another device: no remote copies, remote signals or barrier semaphores. Data moves between devices by JAX's collectives and lax.ppermute only.
A program may use at most 192 MiB of HBM per device.

v0:
```python
import math

import jax
import jax.numpy as jnp
from jax import lax
from jax.experimental import pallas as pl
from jax.experimental.pallas import tpu as pltpu
from jax.sharding import PartitionSpec as P


HD = 128
BLK = 128
K_SEL = 4


SMEM = pl.BlockSpec(memory_space=pltpu.SMEM)
VMEM = pl.BlockSpec(memory_space=pltpu.VMEM)
ANY = pl.BlockSpec(memory_space=pl.ANY)
HBM = pl.BlockSpec(memory_space=pltpu.HBM)


NX, NY, NC = 4, 4, 2


def place_of(group):
    return group // (NY * NC), (group // NC) % NY, group % NC


def steps_of(leg, sign):
    pairs = []
    for group in range(NX * NY * NC):
        x, y, core = place_of(group)
        if (core == 0) == (leg == 0):
            x = (x + sign) % NX
        else:
            y = (y + sign) % NY
        pairs.append((group, (x * NY + y) * NC + core))
    return pairs


def swap_of():
    return [(group, group ^ 1) for group in range(NX * NY * NC)]


def hop(x, leg, sign):
    return lax.ppermute(x, "seq", steps_of(leg, sign))


def swap(x):
    return lax.ppermute(x, "seq", swap_of())


def route(me, entry, port, blocks):
    x, y, core = place_of(me)
    owner_x, owner_y, owner_core = place_of(entry // blocks)
    dx = (owner_x - x + NX) % NX
    dy = (owner_y - y + NY) % NY
    first = jnp.where(core == 0, dx, dy)
    second = jnp.where(core == 0, dy, dx)
    order = jnp.where(first == 0, 0, jnp.where(first == 3, 1, jnp.where(first == 1, 2, 3)))
    return second, order * 4 + 2 * jnp.where(owner_core == core, 0, 1) + port


def fetch(gathered, code, target, sem):
    for kind, source in enumerate(gathered):

        @pl.when(code // 16 == kind)
        def _():
            pltpu.make_async_copy(source.at[code % 16], target, sem).start()


def join_body(*refs):
    out, start = refs[-1], 0
    for ref in refs[:-1]:
        out[start:start + ref.shape[0]] = ref[...]
        start += ref.shape[0]


def pack_body(blocks, lists, me_ref, key, value, mine, other, sems):
    me = me_ref[0]
    core = me % NC
    row = lax.broadcasted_iota(jnp.int32, lists.shape, 1) - me * blocks
    entry = jnp.where((row < 0) | (row >= blocks), lists[...] - me * blocks, -1)
    named = [jnp.max(jnp.where(entry == block, 1.0, 0.0)) > 0.5 for block in range(blocks)]
    first = jnp.where(named[0], 0, jnp.where(named[1], 1, 2))
    second = jnp.where(named[2], 2, jnp.where(named[1], 1, 0))
    for port, block in enumerate((first, second)):
        rows = pl.ds(pl.multiple_of(block * BLK, BLK), BLK)

        @pl.when(core == 0)
        def _():
            pltpu.make_async_copy(key.at[rows], mine.at[port], sems.at[port, 0]).start()
            pltpu.make_async_copy(value.at[rows], other.at[port], sems.at[port, 1]).start()

        @pl.when(core != 0)
        def _():
            pltpu.make_async_copy(value.at[rows], mine.at[port], sems.at[port, 0]).start()
            pltpu.make_async_copy(key.at[rows], other.at[port], sems.at[port, 1]).start()

    for port in range(2):
        rows = pl.ds(0, BLK)
        pltpu.make_async_copy(key.at[rows], mine.at[port], sems.at[port, 0]).wait()
        pltpu.make_async_copy(key.at[rows], other.at[port], sems.at[port, 1]).wait()


def plan_body(blocks, lists, ports, me_ref, table):
    me = me_ref[0]
    far_count = 2 * blocks
    steps = blocks * K_SEL
    spare = table.shape[0] - 1
    partner = me + 1 - 2 * (me % NC)
    for group_index, group in enumerate((me, partner)):
        seen = []
        for block in range(blocks):
            count = jnp.int32(2 * block)
            row = []
            for item in range(K_SEL):
                step = block * K_SEL + item
                entry = lists[item, group * blocks + block]
                place = entry - group * blocks
                far = (place < 0) | (place >= blocks)
                number = count
                distance, index = route(me, entry, ports[entry], blocks)
                kind = jnp.where(index < 8, 0, 4) + jnp.where(
                    distance == 0, 0, jnp.where(distance == 3, 1, jnp.where(distance == 1, 2, 3))
                )
                first = number
                for earlier_entry, earlier_number in reversed(seen):
                    first = jnp.where(earlier_entry == entry, earlier_number, first)
                row.append((entry, number))
                table[jnp.where(far, group_index * far_count + number, spare)] = kind * 16 + index % 8
                table[jnp.where(far, (2 + group_index) * far_count + number, spare)] = jnp.where(first == number, 1, 0)
                if group_index == 0:
                    table[4 * far_count + step] = jnp.where(far, blocks + first, place)
                    table[4 * far_count + steps + step] = jnp.where(far, number, -1)
                count = count + jnp.where(far, 1, 0)
            seen += row


def pick_body(far_count, table, *refs):
    gathered, out, sems = refs[:-2], refs[-2], refs[-1]
    for number in range(far_count):
        fetch(gathered, table[far_count + number], out.at[number], sems.at[number])
    for number in range(far_count):
        pltpu.make_async_copy(gathered[0].at[0], out.at[number], sems.at[number]).wait()


def attend_body(blocks, heads, scale, table, me_ref, query, key, value, grad, swapped, *refs):
    gathered, refs = refs[:8], refs[8:]
    attention, query_grad, near, mine, other, rows_of, totals, sems = refs
    me = me_ref[0]
    core = me % NC
    width = heads * HD
    far_count = 2 * blocks
    steps = blocks * K_SEL

    def start(step, carry):
        block, item = step // K_SEL, step % K_SEL
        slot = table[4 * far_count + step]
        number = table[4 * far_count + steps + step]
        rows = pl.ds(pl.multiple_of(item * BLK, BLK), BLK)

        @pl.when(number < 0)
        def _():
            source = pl.ds(pl.multiple_of(slot * BLK, BLK), BLK)
            pltpu.make_async_copy(key.at[source], rows_of.at[0, block, rows], sems.at[block, item, 0]).start()
            pltpu.make_async_copy(value.at[source], rows_of.at[1, block, rows], sems.at[block, item, 1]).start()

        @pl.when(number >= 0)
        def _():
            fetch(gathered, table[jnp.maximum(number, 0)], rows_of.at[core, block, rows], sems.at[block, item, core])
            pltpu.make_async_copy(
                swapped.at[jnp.maximum(number, 0)], rows_of.at[1 - core, block, rows], sems.at[block, item, 1 - core]
            ).start()

        return carry

    lax.fori_loop(0, steps, start, 0)

    @pl.loop(0, blocks + far_count)
    def _(slot):
        totals[0, slot] = jnp.zeros((BLK, width), jnp.float32)
        totals[1, slot] = jnp.zeros((BLK, width), jnp.float32)

    @pl.loop(0, blocks)
    def _(block):
        for item in range(K_SEL):
            rows = pl.ds(item * BLK, BLK)
            for kind in range(2):
                pltpu.make_async_copy(
                    key.at[pl.ds(0, BLK)], rows_of.at[kind, block, rows], sems.at[block, item, kind]
                ).wait()
        own_rows = pl.ds(pl.multiple_of(block * BLK, BLK), BLK)
        f32, bf16 = jnp.float32, jnp.bfloat16
        every = [pl.ds(head * HD, HD) for head in range(heads)]

        def rows_times_rows(left, right):
            return lax.dot_general(left, right, (((1,), (1,)), ((), ())), preferred_element_type=f32)

        def columns_times(left, right):
            return lax.dot_general(left, right, (((0,), (0,)), ((), ())), preferred_element_type=f32)

        qs = [query[own_rows, columns] for columns in every]
        gs = [grad[own_rows, columns] for columns in every]
        ks = [rows_of[0, block, :, columns] for columns in every]
        vs = [rows_of[1, block, :, columns] for columns in every]
        scores = [rows_times_rows(q, k) * scale for q, k in zip(qs, ks)]
        grad_probs = [rows_times_rows(g, v) for g, v in zip(gs, vs)]
        raised = [jnp.exp(x - jnp.max(x, axis=-1, keepdims=True)) for x in scores]
        probs = [x * (1.0 / jnp.sum(x, axis=-1, keepdims=True)) for x in raised]
        lows = [x.astype(bf16) for x in probs]
        mixed = [jnp.dot(low, v, preferred_element_type=f32).astype(bf16) for low, v in zip(lows, vs)]
        deltas = [jnp.sum(g.astype(f32) * x.astype(f32), axis=-1, keepdims=True) for g, x in zip(gs, mixed)]
        grad_scores = [(p * (x - d)).astype(bf16) for p, x, d in zip(probs, grad_probs, deltas)]
        for head, columns in enumerate(every):
            attention[own_rows, columns] = mixed[head]
            query_grad[own_rows, columns] = (
                jnp.dot(grad_scores[head], ks[head], preferred_element_type=f32) * scale
            ).astype(bf16)
        for head, columns in enumerate(every):
            key_terms = columns_times(grad_scores[head], qs[head]) * scale
            value_terms = columns_times(lows[head], gs[head])
            for item in range(K_SEL):
                slot = table[4 * far_count + block * K_SEL + item]
                part = slice(item * BLK, (item + 1) * BLK)
                totals[0, slot, :, columns] += key_terms[part]
                totals[1, slot, :, columns] += value_terms[part]

    @pl.loop(0, far_count)
    def _(number):
        mine[number] = totals[core, blocks + number].astype(jnp.bfloat16)
        other[number] = totals[1 - core, blocks + number].astype(jnp.bfloat16)

    @pl.loop(0, blocks)
    def _(block):
        rows = pl.ds(pl.multiple_of(block * BLK, BLK), BLK)
        near[0, rows] = totals[0, block]
        near[1, rows] = totals[1, block]


def add_terms(table, mine, theirs, cases):
    far_count = mine.shape[0]
    for group, terms in enumerate((mine, theirs)):

        def body(number, carry):
            code = table[group * far_count + number]
            first = table[(2 + group) * far_count + number] != 0
            for kind, ref in cases:

                @pl.when(first & (code // 16 == kind))
                def _():
                    index = code % 16

                    @pl.loop(0, 4)
                    def _(part):
                        rows = pl.ds(pl.multiple_of(part * (BLK // 4), BLK // 4), BLK // 4)
                        ref[index, rows] = (
                            ref[index, rows].astype(jnp.float32) + terms[number, rows].astype(jnp.float32)
                        ).astype(ref.dtype)

            return carry

        lax.fori_loop(0, far_count, body, 0)


def early_body(table, mine, theirs, far_low, far_high, up, down):
    @pl.loop(0, 8)
    def _(index):
        for ref in (far_low, far_high, up, down):
            ref[index] = jnp.zeros(ref.shape[1:], ref.dtype)

    add_terms(table, mine, theirs, ((3, far_low), (7, far_high), (6, up), (1, down)))


def late_body(table, mine, theirs, from_low, from_high, up, down):
    @pl.loop(0, 8)
    def _(index):
        up[index] = from_low[index]
        down[index] = from_high[index]

    add_terms(table, mine, theirs, ((2, up), (5, down)))


def mid_body(table, mine, theirs, low_first, high_first, low_second, high_second, own, down, up, far_low, far_high, first, second):
    f32, bf16 = jnp.float32, jnp.bfloat16

    @pl.loop(0, 8)
    def _(index):
        first[index] = low_first[index].astype(f32) + high_first[index].astype(f32)
        second[index] = low_second[index].astype(f32) + high_second[index].astype(f32)

    add_terms(table, mine, theirs, ((0, first), (4, second)))

    @pl.loop(0, 4)
    def _(index):
        own[index] = first[index].astype(bf16)
        down[index] = first[index + 4].astype(bf16)
        up[index] = second[index].astype(bf16)

    for index in range(2):
        far_low[index] = second[index + 4].astype(bf16)
        far_high[index] = second[index + 6].astype(bf16)


def turn_body(down, up, from_low, from_high, down_out, up_out):
    f32 = jnp.float32
    up_out[:2] = (up[:2].astype(f32) + from_low[...].astype(f32)).astype(jnp.bfloat16)
    up_out[2:] = up[2:]
    down_out[:2] = down[:2]
    down_out[2:] = (down[2:].astype(f32) + from_high[...].astype(f32)).astype(jnp.bfloat16)


def sum_body(own, from_low, from_high, mine, other):
    f32 = jnp.float32
    total = (own[...].astype(f32) + from_low[...].astype(f32) + from_high[...].astype(f32)).astype(jnp.bfloat16)
    mine[...] = total[:2]
    other[...] = total[2:]


def collect_body(blocks, ports, named, me_ref, near, mine, swapped, key_grad, value_grad):
    me = me_ref[0]
    core = me % NC
    f32 = jnp.float32

    @pl.loop(0, blocks)
    def _(block):
        rows = pl.ds(pl.multiple_of(block * BLK, BLK), BLK)
        port = ports[me * blocks + block]
        weight = named[me * blocks + block] != 0
        for kind, out in enumerate((key_grad, value_grad)):
            term = jnp.where(core == kind, mine[port].astype(f32), swapped[port].astype(f32))
            out[rows] = (near[kind, rows] + jnp.where(weight, term, 0.0)).astype(jnp.bfloat16)


def grad_body(size, me_ref, weight, *refs):
    pieces, (out, held, sems) = refs[:-3], refs[-3:]
    me = me_ref[0]
    width = out.shape[1]
    for number, piece in enumerate(pieces):
        pltpu.make_async_copy(piece, held.at[number], sems.at[number]).start()
    out[...] = jnp.zeros_like(out)

    @pl.loop(0, len(pieces))
    def _(number):
        pltpu.make_async_copy(pieces[0], held.at[number], sems.at[number]).wait()
        half = (number + 1) // 2
        step = jnp.where(number % 2 == 1, size - half, half)
        start = lax.rem(me + step, size) * width
        out[...] += lax.dot_general(
            held[number], weight[:, pl.ds(pl.multiple_of(start, HD), width)],
            (((1,), (1,)), ((), ())), preferred_element_type=jnp.float32,
        )


def half_body(low, high, low_out, high_out, sems):
    cut = low_out.shape[0]
    copies = (
        pltpu.make_async_copy(low.at[pl.ds(0, cut)], low_out, sems.at[0]),
        pltpu.make_async_copy(high.at[pl.ds(cut, cut)], high_out, sems.at[1]),
    )
    for copy in copies:
        copy.start()
    for copy in copies:
        copy.wait()


def grad_end_body(size, me_ref, weight, begun, from_low, from_high, low, high, out):
    me = me_ref[0]
    half = size // 2
    cut, width = low.shape

    def term(piece, step):
        start = lax.rem(me + step, size) * width
        return lax.dot_general(
            piece, weight[:, pl.ds(pl.multiple_of(start, HD), width)],
            (((1,), (1,)), ((), ())), preferred_element_type=jnp.float32,
        )

    total = begun[...] + term(from_low[...], size - half + 1) + term(from_high[...], half - 1)
    for rows, piece in ((slice(0, cut), low), (slice(cut, 2 * cut), high)):
        out[rows] = (total[rows] + term(piece[...], half)).astype(jnp.bfloat16)


def project_body(size, me_ref, attention, weight, *outs):
    me = me_ref[0]
    width = attention.shape[1]

    @pl.loop(0, attention.shape[0] // BLK)
    def _(block):
        rows = pl.ds(pl.multiple_of(block * BLK, BLK), BLK)
        for step, out in enumerate(outs):
            start = lax.rem(me + step, size) * width
            out[rows] = jnp.dot(
                attention[rows], weight[:, pl.ds(pl.multiple_of(start, HD), width)],
                preferred_element_type=jnp.float32,
            ).astype(jnp.bfloat16)


def add(*terms):
    total = terms[0].astype(jnp.float32)
    for term in terms[1:]:
        total = total + term.astype(jnp.float32)
    return total.astype(jnp.bfloat16)


def ring_pair(pair):
    size = lax.axis_size("head")
    out = []
    for x, sign in ((pair[0], 1), (pair[1], -1)):
        out.append(lax.ppermute(x, "head", [(i, (i + sign) % size) for i in range(size)]))
    return tuple(out)


def layer(queries, key_states, value_states, block_lists, out_weight, out_grad):
    size = lax.axis_size("head")
    cells, width = queries.shape
    blocks = cells // BLK
    heads = width // HD
    me = lax.axis_index("seq").reshape(1).astype(jnp.int32)
    column = lax.axis_index("head").reshape(1).astype(jnp.int32)
    bf16, f32 = jnp.bfloat16, jnp.float32
    far = 2 * blocks

    def shape(*dims, dtype=bf16):
        return jax.ShapeDtypeStruct(dims, dtype)

    def call(body, in_specs, out_shape, *operands, out_specs=None, mib=10, scratch=()):
        return pl.pallas_call(
            body,
            in_specs=in_specs,
            out_specs=out_specs or [VMEM] * len(out_shape),
            out_shape=out_shape,
            scratch_shapes=scratch,
            compiler_params=pltpu.CompilerParams(vmem_limit_bytes=mib * 1024 * 1024),
        )(*operands)

    lists = block_lists.T
    piece = shape(2, BLK, width)
    mine, other = call(
        lambda *refs: pack_body(blocks, *refs), [VMEM, SMEM, HBM, HBM], [piece, piece],
        lists, me,
        *(pltpu.with_memory_space_constraint(x, pltpu.HBM) for x in (key_states, value_states)),
        scratch=[pltpu.SemaphoreType.DMA((2, 2))],
    )
    entries = block_lists.reshape(-1)
    entry_group = jnp.arange(entries.shape[0], dtype=jnp.int32) // (blocks * K_SEL)
    far_entry = jnp.where(entries // blocks != entry_group, entries, -1)
    all_blocks = jnp.arange(block_lists.shape[0], dtype=jnp.int32)
    named = jnp.any(far_entry[None, :] == all_blocks[:, None], axis=1).astype(jnp.int32)
    ahead = jnp.concatenate([jnp.zeros((1,), jnp.int32), named[:-1]])
    ahead2 = jnp.concatenate([jnp.zeros((2,), jnp.int32), named[:-2]])
    inner = all_blocks % blocks
    ports = jnp.where(inner == 0, 0, jnp.where(inner == 1, ahead, jnp.maximum(ahead, ahead2)))

    (table,) = call(
        lambda *refs: plan_body(blocks, *refs), [SMEM] * 3,
        [shape(4 * far + 2 * blocks * K_SEL + 1, dtype=jnp.int32)], lists, ports, me, out_specs=[SMEM],
    )

    half = size // 2
    cut = cells // 2
    ring = [(out_grad, out_grad)]
    for _ in range(1, half):
        ring.append(ring_pair(ring[-1]))
    across = ring_pair(call(
        half_body, [HBM] * 2, [shape(cut, width)] * 2, *ring[-1],
        scratch=[pltpu.SemaphoreType.DMA((2,))],
    ))
    pieces = [out_grad]
    for step in range(1, half - 1):
        pieces += ring[step]

    def join(*parts):
        total = sum(part.shape[0] for part in parts)
        return call(join_body, [VMEM] * len(parts), [shape(total, BLK, width)], *parts)[0]

    base = join(mine, swap(other))
    left, right = hop(base, 0, 1), hop(base, 0, -1)
    mid_a = join(base, left)
    low_a, high_a = hop(mid_a, 1, 1), hop(mid_a, 1, -1)
    mid_b = join(right, hop(left[:2], 0, 1), hop(right[2:], 0, -1))
    low_b, high_b = hop(mid_b, 1, 1), hop(mid_b, 1, -1)
    far_a, far_b = hop(low_a, 1, 1), hop(high_b, 1, -1)
    gathered = (mid_a, low_a, high_a, far_a, mid_b, low_b, high_b, far_b)
    (picked,) = call(
        lambda *refs: pick_body(far, *refs), [SMEM] + [ANY] * 8, [shape(far, BLK, width)],
        table, *gathered, scratch=[pltpu.SemaphoreType.DMA((far,))],
    )
    swapped = swap(picked)
    (begun,) = call(
        lambda *refs: grad_body(size, *refs), [SMEM, VMEM] + [HBM] * len(pieces),
        [shape(cells, width, dtype=f32)], column, out_weight, *pieces,
        scratch=[pltpu.VMEM((len(pieces), cells, width), bf16), pltpu.SemaphoreType.DMA((len(pieces),))],
    )
    (grad_attn,) = call(
        lambda *refs: grad_end_body(size, *refs), [SMEM] + [VMEM] * 6, [shape(cells, width)],
        column, out_weight, begun, *ring[-1], *across,
    )
    attention, query_grad, near, terms, terms_other = call(
        lambda *refs: attend_body(blocks, heads, 1.0 / math.sqrt(HD), *refs),
        [SMEM, SMEM, VMEM, ANY, ANY, VMEM] + [ANY] * 9,
        [
            shape(cells, width), shape(cells, width), shape(2, cells, width, dtype=f32),
            shape(far, BLK, width), shape(far, BLK, width),
        ],
        table, me, queries, key_states, value_states, grad_attn, swapped, *gathered,
        scratch=[
            pltpu.VMEM((2, blocks, K_SEL * BLK, width), bf16),
            pltpu.VMEM((2, blocks + far, BLK, width), f32),
            pltpu.SemaphoreType.DMA((blocks, K_SEL, 2)),
        ],
        mib=16,
    )
    theirs = swap(terms_other)
    parts = call(
        lambda *refs: project_body(size, *refs), [SMEM, VMEM, VMEM], [shape(cells, width)] * size,
        column, attention, out_weight,
    )
    lead = (table, terms, theirs)
    lead_specs = [SMEM, VMEM, VMEM]
    eight = shape(8, BLK, width)
    far_low, far_high, up_b, down_a = call(early_body, lead_specs, [eight] * 4, *lead)
    from_low, from_high = hop(far_low, 1, 1), hop(far_high, 1, -1)
    low_b, high_a = hop(up_b, 1, 1), hop(down_a, 1, -1)
    ahead, back = ring_pair((parts[half][:cut], parts[half][cut:]))
    up_a, down_b = call(late_body, lead_specs + [VMEM] * 2, [eight] * 2, *lead, from_low, from_high)
    low_a, high_b = hop(up_a, 1, 1), hop(down_b, 1, -1)
    ahead = jnp.concatenate([add(parts[half - 1][:cut], ahead), parts[half - 1][cut:]])
    back = jnp.concatenate([parts[half + 1][:cut], add(parts[half + 1][cut:], back)])
    for distance in range(half - 2, -1, -1):
        ahead, back = ring_pair((ahead, back))
        if distance:
            ahead, back = add(parts[distance], ahead), add(parts[size - distance], back)
    attended = add(parts[0], ahead, back)
    own, down, up, far_low, far_high = call(
        mid_body, lead_specs + [VMEM] * 4, [shape(4, BLK, width)] * 3 + [piece] * 2,
        *lead, low_a, high_a, low_b, high_b,
        scratch=[pltpu.VMEM((8, BLK, width), f32)] * 2,
    )
    down, up = call(
        turn_body, [VMEM] * 4, [shape(4, BLK, width)] * 2,
        down, up, hop(far_low, 0, 1), hop(far_high, 0, -1),
    )
    mine, other = call(sum_body, [VMEM] * 3, [piece, piece], own, hop(up, 0, 1), hop(down, 0, -1))
    key_grad, value_grad = call(
        lambda *refs: collect_body(blocks, *refs), [SMEM, SMEM, SMEM] + [VMEM] * 3,
        [shape(cells, width)] * 2,
        ports, named, me, near, mine, swap(other),
    )
    return attended, query_grad, key_grad, value_grad


def solution(mesh):
    in_specs = (
        P("seq", "head"),
        P("seq", "head"),
        P("seq", "head"),
        P(),
        P("head", None),
        P("seq", "head"),
    )
    out_specs = (P("seq", "head"), P("seq", "head"), P("seq", "head"), P("seq", "head"))
    return jax.shard_map(layer, mesh=mesh, in_specs=in_specs, out_specs=out_specs, check_vma=False)
```

profile of v0, /device:TPU:8, one launch (start us, length us, event | category | flops | bytes accessed | tf_op | source)
XLA Modules:
  0.0 158.1 jit_solution(11417101057346901713)
XLA Ops:
  0.6 0.7 copy-done.17
  1.3 1.2 shard_map.97
  2.6 1.4 collective-permute-done.8.refs_1_
  4.1 2.8 %collective-permute-start.13 = (bf16[4,128,384]{2,1,0:T(8,128)(2,1)S(1)}, bf16[4,128,384]{2,1,0:T(8,128)(2,1)S(1)}, u32[]{:S(2)}, u32[]{:S(2)}) collective-permute-start(bf16[4,128,384]{2,1,0:T(8,128)(2,1)S(1)} %shard_map.98.refs_0_), channel_id=1, source_target_pairs={{0,192},{8,56},{16,208},{24,8},{32,224},{40,24},{48,240},{56,40},{... | collective-permute-start | bytes 1179656 | tf_op jit(solution)/shard_map/ppermute | solution.py:46
  6.9 5.3 %collective-permute-done.13.refs_0_ = bf16[4,128,384]{2,1,0:T(8,128)(2,1)S(1)} collective-permute-done((bf16[4,128,384]{2,1,0:T(8,128)(2,1)S(1)}, bf16[4,128,384]{2,1,0:T(8,128)(2,1)S(1)}, u32[]{:S(2)}, u32[]{:S(2)}) %collective-permute-start.13) | collective-permute-done | bytes 393248 | tf_op jit(solution)/shard_map/ppermute | solution.py:46
  12.3 3.8 %collective-permute-start.15 = (bf16[2,128,384]{2,1,0:T(8,128)(2,1)S(1)}, bf16[2,128,384]{2,1,0:T(8,128)(2,1)S(1)}, u32[]{:S(2)}, u32[]{:S(2)}) collective-permute-start(bf16[2,128,384]{2,1,0:T(8,128)(2,1)S(1)} %slice.41), channel_id=1, source_target_pairs={{0,192},{8,56},{16,208},{24,8},{32,224},{40,24},{48,240},{56,40},{... | collective-permute-start | bytes 589832 | tf_op jit(solution)/shard_map/ppermute | solution.py:46
  16.2 1.7 %collective-permute-start.10 = (bf16[8,128,384]{2,1,0:T(8,128)(2,1)S(1)}, bf16[8,128,384]{2,1,0:T(8,128)(2,1)}, u32[]{:S(2)}, u32[]{:S(2)}) collective-permute-start(bf16[8,128,384]{2,1,0:T(8,128)(2,1)S(1)} %shard_map.99.refs_1_.refs_7_), channel_id=1, source_target_pairs={{0,16},{8,72},{16,32},{24,88},{32,48},{40,104},{48,0},{56,120},{64... | collective-permute-start | bytes 2359304 | tf_op jit(solution)/shard_map/ppermute | solution.py:46
  17.9 1.3 collective-permute-done.15.refs_2_
  19.2 5.9 %collective-permute-done.14.refs_1_ = bf16[2,128,384]{2,1,0:T(8,128)(2,1)S(1)} collective-permute-done((bf16[2,128,384]{2,1,0:T(8,128)(2,1)S(1)}, bf16[2,128,384]{2,1,0:T(8,128)(2,1)S(1)}, u32[]{:S(2)}, u32[]{:S(2)}) %collective-permute-start.14) | collective-permute-done | bytes 196640 | tf_op jit(solution)/shard_map/ppermute | solution.py:46
  25.1 0.9 shard_map.100.refs_5_.refs_11_
  26.1 0.5 collective-permute-start.17
  26.5 3.0 %collective-permute-start.11 = (bf16[8,128,384]{2,1,0:T(8,128)(2,1)S(1)}, bf16[8,128,384]{2,1,0:T(8,128)(2,1)S(1)}, u32[]{:S(2)}, u32[]{:S(2)}) collective-permute-start(bf16[8,128,384]{2,1,0:T(8,128)(2,1)S(1)} %shard_map.99.refs_1_.refs_7_), channel_id=1, source_target_pairs={{0,48},{8,200},{16,0},{24,216},{32,16},{40,232},{48,32},{56,248},{... | collective-permute-start | bytes 2359304 | tf_op jit(solution)/shard_map/ppermute | solution.py:46
  29.5 1.9 %collective-permute-start = (bf16[384,384]{1,0:T(8,128)(2,1)S(1)}, bf16[384,384]{1,0:T(8,128)(2,1)S(1)}, u32[]{:S(2)}, u32[]{:S(2)}) collective-permute-start(bf16[384,384]{1,0:T(8,128)(2,1)S(1)} %copy-done.8), channel_id=1, source_target_pairs={{0,1},{1,2},{2,3},{3,4},{4,5},{5,6},{6,7},{7,0},{8,9},{9,10},{10,1... | collective-permute-start | bytes 884744 | tf_op jit(solution)/shard_map/ppermute | solution.py:410
  31.5 0.6 collective-permute-start.12
  32.0 6.3 %collective-permute-done.17.refs_7_.refs_13_ = bf16[8,128,384]{2,1,0:T(8,128)(2,1)} collective-permute-done((bf16[8,128,384]{2,1,0:T(8,128)(2,1)}, bf16[8,128,384]{2,1,0:T(8,128)(2,1)}, u32[]{:S(2)}, u32[]{:S(2)}) %collective-permute-start.17) | collective-permute-done | bytes 786464 | tf_op jit(solution)/shard_map/ppermute | solution.py:46
  38.4 1.0 collective-permute-start.18
  39.4 0.7 collective-permute-done.refs_3_
  40.1 5.1 %collective-permute-start.1 = (bf16[384,384]{1,0:T(8,128)(2,1)S(1)}, bf16[384,384]{1,0:T(8,128)(2,1)}, u32[]{:S(2)}, u32[]{:S(2)}) collective-permute-start(bf16[384,384]{1,0:T(8,128)(2,1)S(1)} %copy-done.8), channel_id=1, source_target_pairs={{0,7},{1,0},{2,1},{3,2},{4,3},{5,4},{6,5},{7,6},{8,15},{9,8},{10,9... | collective-permute-start | bytes 884744 | tf_op jit(solution)/shard_map/ppermute | solution.py:410
  45.4 4.0 %collective-permute-done.1.refs_4_ = bf16[384,384]{1,0:T(8,128)(2,1)} collective-permute-done((bf16[384,384]{1,0:T(8,128)(2,1)S(1)}, bf16[384,384]{1,0:T(8,128)(2,1)}, u32[]{:S(2)}, u32[]{:S(2)}) %collective-permute-start.1) | collective-permute-done | bytes 294944 | tf_op jit(solution)/shard_map/ppermute | solution.py:410
  49.5 0.7 copy-done.11
  50.2 0.9 copy-done.1
  51.1 3.8 %collective-permute-start.3 = (bf16[384,384]{1,0:T(8,128)(2,1)}, bf16[384,384]{1,0:T(8,128)(2,1)S(1)}, u32[]{:S(2)}, u32[]{:S(2)}) collective-permute-start(bf16[384,384]{1,0:T(8,128)(2,1)} %collective-permute-done.1.refs_4_), channel_id=1, source_target_pairs={{0,7},{1,0},{2,1},{3,2},{4,3},{5,4},{6,5},{7,6},{8,15},{9,8},{10,9... | collective-permute-start | bytes 884744 | tf_op jit(solution)/shard_map/ppermute | solution.py:410
  55.1 2.2 %shard_map.93.refs_0_.table = s32[49]{0:T(128)S(1)} custom-call(s32[4,96]{1,0:T(4,128)S(1)} %bitcast.6, s32[96]{0:T(128)S(1)} %compare_select_fusion.1.refs_1_.refs_0_, s32[1]{0:T(128)} %bitcast.2.refs_2_.refs_1_), custom_call_target="tpu_custom_call" | custom-call | tf_op jit(solution)/shard_map/pallas_call | solution.py:428
  57.4 1.3 copy-done.2
  58.6 2.8 %shard_map.101 = bf16[6,128,384]{2,1,0:T(8,128)(2,1)} custom-call(s32[49]{0:T(128)S(1)} %shard_map.93.refs_0_.table, bf16[8,128,384]{2,1,0:T(8,128)(2,1)S(1)} %shard_map.99.refs_1_.refs_7_, bf16[8,128,384]{2,1,0:T(8,128)(2,1)} %collective-permute-done.10.refs_2_.refs_8_, bf16[8,128,384]{2,1,0:T(8,128)(2,1)S(1)} %copy-done.2, ...), custom_call_target="tpu_custom_call" | custom-call | tf_op jit(solution)/shard_map/pallas_call | solution.py:428
  61.7 3.6 %collective-permute-start.5 = (bf16[384,384]{1,0:T(8,128)(2,1)S(1)}, bf16[384,384]{1,0:T(8,128)(2,1)S(1)}, u32[]{:S(2)}, u32[]{:S(2)}) collective-permute-start(bf16[384,384]{1,0:T(8,128)(2,1)S(1)} %collective-permute-done.3.refs_6_), channel_id=1, source_target_pairs={{0,7},{1,0},{2,1},{3,2},{4,3},{5,4},{6,5},{7,6},{8,15},{9,8},{10,9... | collective-permute-start | bytes 884744 | tf_op jit(solution)/shard_map/ppermute | solution.py:410
  65.3 7.5 %collective-permute-done.4.low.refs_3_ = bf16[384,384]{1,0:T(8,128)(2,1)S(1)} collective-permute-done((bf16[384,384]{1,0:T(8,128)(2,1)S(1)}, bf16[384,384]{1,0:T(8,128)(2,1)S(1)}, u32[]{:S(2)}, u32[]{:S(2)}) %collective-permute-start.4) | collective-permute-done | bytes 294944 | tf_op jit(solution)/shard_map/ppermute | solution.py:410
  72.8 1.1 shard_map.95
  73.9 0.7 copy-done.4
  74.6 3.2 %collective-permute-start.7 = (bf16[192,384]{1,0:T(8,128)(2,1)}, bf16[192,384]{1,0:T(8,128)(2,1)}, u32[]{:S(2)}, u32[]{:S(2)}) collective-permute-start(bf16[192,384]{1,0:T(8,128)(2,1)} %get-tuple-element.39), channel_id=1, source_target_pairs={{0,7},{1,0},{2,1},{3,2},{4,3},{5,4},{6,5},{7,6},{8,15},{9,8},{10,9... | collective-permute-start | bytes 442376 | tf_op jit(solution)/shard_map/ppermute | solution.py:410
  77.9 1.0 copy-done.9
  78.9 1.0 copy-done.12
  79.8 1.0 copy-done.14
  80.8 1.0 copy-done.16
  81.8 2.2 %shard_map.94.refs_2_ = f32[384,384]{1,0:T(8,128)S(1)} custom-call(s32[1]{0:T(128)} %bitcast.refs_0_, bf16[384,3072]{1,0:T(8,128)(2,1)S(1)} %copy-done, bf16[384,384]{1,0:T(8,128)(2,1)S(1)} %copy-done.9, bf16[384,384]{1,0:T(8,128)(2,1)S(1)} %copy-done.12, bf16[384,384]{1,0:T(8,128)(2,1)} %collective-permute-done.1.refs_4_, bf16[384,384]{1,0:T(8,128)(2,1)S(1)} %copy-done.14, ...), custom_call_target="tpu_custom_call" | custom-call | tf_op jit(solution)/shard_map/pallas_call | solution.py:428
  84.1 1.8 %shard_map.96.refs_5_ = bf16[384,384]{1,0:T(8,128)(2,1)S(1)} custom-call(s32[1]{0:T(128)} %bitcast.refs_0_, bf16[384,3072]{1,0:T(8,128)(2,1)S(1)} %copy-done, f32[384,384]{1,0:T(8,128)S(1)} %shard_map.94.refs_2_, bf16[384,384]{1,0:T(8,128)(2,1)S(1)} %collective-permute-done.4.low.refs_3_, bf16[384,384]{1,0:T(8,128)(2,1)S(1)} %copy-done.5, ...), custom_call_target="tpu_custom_call" | custom-call | tf_op jit(solution)/shard_map/pallas_call | solution.py:428
  86.0 7.8 %shard_map.102 = (bf16[384,384]{1,0:T(8,128)(2,1)S(1)}, bf16[384,384]{1,0:T(8,128)(2,1)}, f32[2,384,384]{2,1,0:T(8,128)S(1)}, bf16[6,128,384]{2,1,0:T(8,128)(2,1)S(1)}, bf16[6,128,384]{2,1,0:T(8,128)(2,1)S(1)}) custom-call(s32[49]{0:T(128)S(1)} %shard_map.93.refs_0_.table, s32[1]{0:T(128)} %bitcast.2.refs_2_.refs_1_, bf16[384,384]{1,0:T(8,128)(2,1)S(1)} %copy-done.10, ...), custom_call_target="tpu_custom_call" | custom-call | tf_op jit(solution)/shard_map/pallas_call | solution.py:428
  93.9 2.0 %collective-permute-done.28.theirs = bf16[6,128,384]{2,1,0:T(8,128)(2,1)S(1)} collective-permute-done((bf16[6,128,384]{2,1,0:T(8,128)(2,1)S(1)}, bf16[6,128,384]{2,1,0:T(8,128)(2,1)S(1)}, u32[]{:S(2)}, u32[]{:S(2)}) %collective-permute-start.28) | collective-permute-done | bytes 589856 | tf_op jit(solution)/shard_map/ppermute | solution.py:50
  95.9 1.5 shard_map.104
  97.4 2.2 %collective-permute-start.29 = (bf16[8,128,384]{2,1,0:T(8,128)(2,1)S(1)}, bf16[8,128,384]{2,1,0:T(8,128)(2,1)S(1)}, u32[]{:S(2)}, u32[]{:S(2)}) collective-permute-start(bf16[8,128,384]{2,1,0:T(8,128)(2,1)S(1)} %get-tuple-element.55), channel_id=1, source_target_pairs={{0,16},{8,72},{16,32},{24,88},{32,48},{40,104},{48,0},{56,120},{64... | collective-permute-start | bytes 2359304 | tf_op jit(solution)/shard_map/ppermute | solution.py:46
  99.6 1.6 %collective-permute-start.30 = (bf16[8,128,384]{2,1,0:T(8,128)(2,1)S(1)}, bf16[8,128,384]{2,1,0:T(8,128)(2,1)S(1)}, u32[]{:S(2)}, u32[]{:S(2)}) collective-permute-start(bf16[8,128,384]{2,1,0:T(8,128)(2,1)S(1)} %get-tuple-element.56), channel_id=1, source_target_pairs={{0,48},{8,200},{16,0},{24,216},{32,16},{40,232},{48,32},{56,248},{... | collective-permute-start | bytes 2359304 | tf_op jit(solution)/shard_map/ppermute | solution.py:46
  101.2 2.1 %shard_map.103 = (bf16[384,384]{1,0:T(8,128)(2,1)S(1)}, bf16[384,384]{1,0:T(8,128)(2,1)S(1)}, bf16[384,384]{1,0:T(8,128)(2,1)S(1)}, bf16[384,384]{1,0:T(8,128)(2...) custom-call(s32[1]{0:T(128)} %bitcast.refs_0_, ...), custom_call_target="tpu_custom_call" | custom-call | tf_op jit(solution)/shard_map/pallas_call | solution.py:428
  103.4 1.8 %collective-permute-start.24 = (bf16[192,384]{1,0:T(8,128)(2,1)S(1)}, bf16[192,384]{1,0:T(8,128)(2,1)S(1)}, u32[]{:S(2)}, u32[]{:S(2)}) collective-permute-start(bf16[192,384]{1,0:T(8,128)(2,1)S(1)} %get-tuple-element.73), channel_id=1, source_target_pairs={{0,7},{1,0},{2,1},{3,2},{4,3},{5,4},{6,5},{7,6},{8,15},{9,8},{10,9... | collective-permute-start | bytes 442376 | tf_op jit(solution)/shard_map/ppermute | solution.py:410
  105.2 0.3 collective-permute-start.20
  105.6 3.0 %collective-permute-done.24 = bf16[192,384]{1,0:T(8,128)(2,1)S(1)} collective-permute-done((bf16[192,384]{1,0:T(8,128)(2,1)S(1)}, bf16[192,384]{1,0:T(8,128)(2,1)S(1)}, u32[]{:S(2)}, u32[]{:S(2)}) %collective-permute-start.24) | collective-permute-done | bytes 147488 | tf_op jit(solution)/shard_map/ppermute | solution.py:410
  108.7 3.3 %collective-permute-start.25 = (bf16[384,384]{1,0:T(8,128)(2,1)S(1)}, bf16[384,384]{1,0:T(8,128)(2,1)S(1)}, u32[]{:S(2)}, u32[]{:S(2)}) collective-permute-start(bf16[384,384]{1,0:T(8,128)(2,1)S(1)} %pad_maximum_fusion.1), channel_id=1, source_target_pairs={{0,7},{1,0},{2,1},{3,2},{4,3},{5,4},{6,5},{7,6},{8,15},{9,8},{10,9... | collective-permute-start | bytes 884744 | tf_op jit(solution)/shard_map/ppermute | solution.py:410
  111.9 3.2 %collective-permute-start.32 = (bf16[8,128,384]{2,1,0:T(8,128)(2,1)S(1)}, bf16[8,128,384]{2,1,0:T(8,128)(2,1)S(1)}, u32[]{:S(2)}, u32[]{:S(2)}) collective-permute-start(bf16[8,128,384]{2,1,0:T(8,128)(2,1)S(1)} %get-tuple-element.58), channel_id=1, source_target_pairs={{0,48},{8,200},{16,0},{24,216},{32,16},{40,232},{48,32},{56,248},{... | collective-permute-start | bytes 2359304 | tf_op jit(solution)/shard_map/ppermute | solution.py:46
  115.2 1.2 shard_map.105
  116.4 0.9 collective-permute-start.31
  117.3 1.3 collective-permute-start.34
  118.9 7.8 %collective-permute-done.21 = bf16[384,384]{1,0:T(8,128)(2,1)S(1)} collective-permute-done((bf16[384,384]{1,0:T(8,128)(2,1)S(1)}, bf16[384,384]{1,0:T(8,128)(2,1)S(1)}, u32[]{:S(2)}, u32[]{:S(2)}) %collective-permute-start.21) | collective-permute-done | bytes 294944 | tf_op jit(solution)/shard_map/ppermute | solution.py:410
  126.7 0.6 collective-permute-start.26
  127.4 1.5 collective-permute-start.22
  128.9 6.7 %collective-permute-done.31.low_first = bf16[8,128,384]{2,1,0:T(8,128)(2,1)S(1)} collective-permute-done((bf16[8,128,384]{2,1,0:T(8,128)(2,1)S(1)}, bf16[8,128,384]{2,1,0:T(8,128)(2,1)S(1)}, u32[]{:S(2)}, u32[]{:S(2)}) %collective-permute-start.31) | collective-permute-done | bytes 786464 | tf_op jit(solution)/shard_map/ppermute | solution.py:46
  135.6 1.5 shard_map.106
  137.2 3.2 %collective-permute-start.36 = (bf16[2,128,384]{2,1,0:T(8,128)(2,1)S(1)}, bf16[2,128,384]{2,1,0:T(8,128)(2,1)S(1)}, u32[]{:S(2)}, u32[]{:S(2)}) collective-permute-start(bf16[2,128,384]{2,1,0:T(8,128)(2,1)S(1)} %get-tuple-element.65), channel_id=1, source_target_pairs={{0,192},{8,56},{16,208},{24,8},{32,224},{40,24},{48,240},{56,40},{... | collective-permute-start | bytes 589832 | tf_op jit(solution)/shard_map/ppermute | solution.py:46
  140.5 0.2 collective-permute-start.27
  140.6 3.4 %collective-permute-done.35.from_low = bf16[2,128,384]{2,1,0:T(8,128)(2,1)S(1)} collective-permute-done((bf16[2,128,384]{2,1,0:T(8,128)(2,1)S(1)}, bf16[2,128,384]{2,1,0:T(8,128)(2,1)S(1)}, u32[]{:S(2)}, u32[]{:S(2)}) %collective-permute-start.35) | collective-permute-done | bytes 196640 | tf_op jit(solution)/shard_map/ppermute | solution.py:46
  144.2 3.3 %collective-permute-start.38 = (bf16[4,128,384]{2,1,0:T(8,128)(2,1)S(1)}, bf16[4,128,384]{2,1,0:T(8,128)(2,1)S(1)}, u32[]{:S(2)}, u32[]{:S(2)}) collective-permute-start(bf16[4,128,384]{2,1,0:T(8,128)(2,1)S(1)} %get-tuple-element.67), channel_id=1, source_target_pairs={{0,192},{8,56},{16,208},{24,8},{32,224},{40,24},{48,240},{56,40},{... | collective-permute-start | bytes 1179656 | tf_op jit(solution)/shard_map/ppermute | solution.py:46
  147.7 5.5 %collective-permute-done.37.from_low = bf16[4,128,384]{2,1,0:T(8,128)(2,1)S(1)} collective-permute-done((bf16[4,128,384]{2,1,0:T(8,128)(2,1)S(1)}, bf16[4,128,384]{2,1,0:T(8,128)(2,1)S(1)}, u32[]{:S(2)}, u32[]{:S(2)}) %collective-permute-start.37) | collective-permute-done | bytes 393248 | tf_op jit(solution)/shard_map/ppermute | solution.py:46
  153.2 0.1 shard_map.108
  153.5 2.2 %collective-permute-done.23 = bf16[384,384]{1,0:T(8,128)(2,1)S(1)} collective-permute-done((bf16[384,384]{1,0:T(8,128)(2,1)S(1)}, bf16[384,384]{1,0:T(8,128)(2,1)S(1)}, u32[]{:S(2)}, u32[]{:S(2)}) %collective-permute-start.23) | collective-permute-done | bytes 294944 | tf_op jit(solution)/shard_map/ppermute | solution.py:410
  155.7 0.8 add_convert_fusion
  156.5 1.6 shard_map.109
  (91 shorter events, 2.2 us)
Async XLA Ops:
  0.6 0.7 copy-start.17
  2.5 1.5 collective-permute-start.8
  4.1 25.5 %copy-start.8 = (bf16[384,384]{1,0:T(8,128)(2,1)S(1)}, bf16[384,384]{1,0:T(8,128)(2,1)}, u32[]{:S(2)}) copy-start(bf16[384,384]{1,0:T(8,128)(2,1)} %refs_2_.4) | copy-start | bytes 884740
  4.1 41.2 %copy-start.18 = (s32[96,4]{0,1:T(4,128)S(1)}, s32[96,4]{0,1:T(4,128)}, u32[]{:S(2)}) copy-start(s32[96,4]{0,1:T(4,128)} %param.9) | copy-start | bytes 4612
  4.1 8.1 %collective-permute-start.13 = (bf16[4,128,384]{2,1,0:T(8,128)(2,1)S(1)}, bf16[4,128,384]{2,1,0:T(8,128)(2,1)S(1)}, u32[]{:S(2)}, u32[]{:S(2)}) collective-permute-start(bf16[4,128,384]{2,1,0:T(8,128)(2,1)S(1)} %shard_map.98.refs_0_), channel_id=1, source_target_pairs={{0,192},{8,56},{16,208},{24,8},{32,224},{40,24},{48,240},{56,40},{... | collective-permute-start | bytes 1179656 | tf_op jit(solution)/shard_map/ppermute | solution.py:46
  6.9 9.1 %collective-permute-start.9 = (bf16[4,128,384]{2,1,0:T(8,128)(2,1)S(1)}, bf16[4,128,384]{2,1,0:T(8,128)(2,1)S(1)}, u32[]{:S(2)}, u32[]{:S(2)}) collective-permute-start(bf16[4,128,384]{2,1,0:T(8,128)(2,1)S(1)} %shard_map.98.refs_0_), channel_id=1, source_target_pairs={{0,64},{8,24},{16,80},{24,40},{32,96},{40,56},{48,112},{56,8},{64,... | collective-permute-start | bytes 1179656 | tf_op jit(solution)/shard_map/ppermute | solution.py:46
  12.3 7.0 %collective-permute-start.15 = (bf16[2,128,384]{2,1,0:T(8,128)(2,1)S(1)}, bf16[2,128,384]{2,1,0:T(8,128)(2,1)S(1)}, u32[]{:S(2)}, u32[]{:S(2)}) collective-permute-start(bf16[2,128,384]{2,1,0:T(8,128)(2,1)S(1)} %slice.41), channel_id=1, source_target_pairs={{0,192},{8,56},{16,208},{24,8},{32,224},{40,24},{48,240},{56,40},{... | collective-permute-start | bytes 589832 | tf_op jit(solution)/shard_map/ppermute | solution.py:46
  16.1 9.1 %collective-permute-start.14 = (bf16[2,128,384]{2,1,0:T(8,128)(2,1)S(1)}, bf16[2,128,384]{2,1,0:T(8,128)(2,1)S(1)}, u32[]{:S(2)}, u32[]{:S(2)}) collective-permute-start(bf16[2,128,384]{2,1,0:T(8,128)(2,1)S(1)} %slice.40), channel_id=1, source_target_pairs={{0,64},{8,24},{16,80},{24,40},{32,96},{40,56},{48,112},{56,8},{64,... | collective-permute-start | bytes 589832 | tf_op jit(solution)/shard_map/ppermute | solution.py:46
  16.2 15.2 %collective-permute-start.10 = (bf16[8,128,384]{2,1,0:T(8,128)(2,1)S(1)}, bf16[8,128,384]{2,1,0:T(8,128)(2,1)}, u32[]{:S(2)}, u32[]{:S(2)}) collective-permute-start(bf16[8,128,384]{2,1,0:T(8,128)(2,1)S(1)} %shard_map.99.refs_1_.refs_7_), channel_id=1, source_target_pairs={{0,16},{8,72},{16,32},{24,88},{32,48},{40,104},{48,0},{56,120},{64... | collective-permute-start | bytes 2359304 | tf_op jit(solution)/shard_map/ppermute | solution.py:46
  26.1 12.3 %collective-permute-start.17 = (bf16[8,128,384]{2,1,0:T(8,128)(2,1)}, bf16[8,128,384]{2,1,0:T(8,128)(2,1)}, u32[]{:S(2)}, u32[]{:S(2)}) collective-permute-start(bf16[8,128,384]{2,1,0:T(8,128)(2,1)} %shard_map.100.refs_5_.refs_11_), channel_id=1, source_target_pairs={{0,48},{8,200},{16,0},{24,216},{32,16},{40,232},{48,32},{56,248},{... | collective-permute-start | bytes 2359304 | tf_op jit(solution)/shard_map/ppermute | solution.py:46
  26.5 23.7 %collective-permute-start.11 = (bf16[8,128,384]{2,1,0:T(8,128)(2,1)S(1)}, bf16[8,128,384]{2,1,0:T(8,128)(2,1)S(1)}, u32[]{:S(2)}, u32[]{:S(2)}) collective-permute-start(bf16[8,128,384]{2,1,0:T(8,128)(2,1)S(1)} %shard_map.99.refs_1_.refs_7_), channel_id=1, source_target_pairs={{0,48},{8,200},{16,0},{24,216},{32,16},{40,232},{48,32},{56,248},{... | collective-permute-start | bytes 2359304 | tf_op jit(solution)/shard_map/ppermute | solution.py:46
  29.5 10.6 %collective-permute-start = (bf16[384,384]{1,0:T(8,128)(2,1)S(1)}, bf16[384,384]{1,0:T(8,128)(2,1)S(1)}, u32[]{:S(2)}, u32[]{:S(2)}) collective-permute-start(bf16[384,384]{1,0:T(8,128)(2,1)S(1)} %copy-done.8), channel_id=1, source_target_pairs={{0,1},{1,2},{2,3},{3,4},{4,5},{5,6},{6,7},{7,0},{8,9},{9,10},{10,1... | collective-permute-start | bytes 884744 | tf_op jit(solution)/shard_map/ppermute | solution.py:410
  31.4 25.9 %collective-permute-start.16 = (bf16[8,128,384]{2,1,0:T(8,128)(2,1)}, bf16[8,128,384]{2,1,0:T(8,128)(2,1)}, u32[]{:S(2)}, u32[]{:S(2)}) collective-permute-start(bf16[8,128,384]{2,1,0:T(8,128)(2,1)} %shard_map.100.refs_5_.refs_11_), channel_id=1, source_target_pairs={{0,16},{8,72},{16,32},{24,88},{32,48},{40,104},{48,0},{56,120},{64... | collective-permute-start | bytes 2359304 | tf_op jit(solution)/shard_map/ppermute | solution.py:46
  31.5 25.9 %collective-permute-start.12 = (bf16[8,128,384]{2,1,0:T(8,128)(2,1)}, bf16[8,128,384]{2,1,0:T(8,128)(2,1)}, u32[]{:S(2)}, u32[]{:S(2)}) collective-permute-start(bf16[8,128,384]{2,1,0:T(8,128)(2,1)} %collective-permute-done.10.refs_2_.refs_8_), channel_id=1, source_target_pairs={{0,16},{8,72},{16,32},{24,88},{32,48},{40,104},{48,0},{56,120},{64... | collective-permute-start | bytes 2359304 | tf_op jit(solution)/shard_map/ppermute | solution.py:46
  38.4 19.0 %collective-permute-start.18 = (bf16[8,128,384]{2,1,0:T(8,128)(2,1)}, bf16[8,128,384]{2,1,0:T(8,128)(2,1)}, u32[]{:S(2)}, u32[]{:S(2)}) collective-permute-start(bf16[8,128,384]{2,1,0:T(8,128)(2,1)} %collective-permute-done.17.refs_7_.refs_13_), channel_id=1, source_target_pairs={{0,48},{8,200},{16,0},{24,216},{32,16},{40,232},{48,32},{56,248},{... | collective-permute-start | bytes 2359304 | tf_op jit(solution)/shard_map/ppermute | solution.py:46
  40.1 9.4 %collective-permute-start.1 = (bf16[384,384]{1,0:T(8,128)(2,1)S(1)}, bf16[384,384]{1,0:T(8,128)(2,1)}, u32[]{:S(2)}, u32[]{:S(2)}) collective-permute-start(bf16[384,384]{1,0:T(8,128)(2,1)S(1)} %copy-done.8), channel_id=1, source_target_pairs={{0,7},{1,0},{2,1},{3,2},{4,3},{5,4},{6,5},{7,6},{8,15},{9,8},{10,9... | collective-permute-start | bytes 884744 | tf_op jit(solution)/shard_map/ppermute | solution.py:410
  49.5 12.1 %collective-permute-start.2 = (bf16[384,384]{1,0:T(8,128)(2,1)S(1)}, bf16[384,384]{1,0:T(8,128)(2,1)S(1)}, u32[]{:S(2)}, u32[]{:S(2)}) collective-permute-start(bf16[384,384]{1,0:T(8,128)(2,1)S(1)} %collective-permute-done.refs_3_), channel_id=1, source_target_pairs={{0,1},{1,2},{2,3},{3,4},{4,5},{5,6},{6,7},{7,0},{8,9},{9,10},{10,1... | collective-permute-start | bytes 884744 | tf_op jit(solution)/shard_map/ppermute | solution.py:410
  49.5 0.7 copy-start.11
  50.2 0.9 copy-start.1
  51.1 10.6 %collective-permute-start.3 = (bf16[384,384]{1,0:T(8,128)(2,1)}, bf16[384,384]{1,0:T(8,128)(2,1)S(1)}, u32[]{:S(2)}, u32[]{:S(2)}) collective-permute-start(bf16[384,384]{1,0:T(8,128)(2,1)} %collective-permute-done.1.refs_4_), channel_id=1, source_target_pairs={{0,7},{1,0},{2,1},{3,2},{4,3},{5,4},{6,5},{7,6},{8,15},{9,8},{10,9... | collective-permute-start | bytes 884744 | tf_op jit(solution)/shard_map/ppermute | solution.py:410
  57.3 20.6 %copy-start = (bf16[384,3072]{1,0:T(8,128)(2,1)S(1)}, bf16[384,3072]{1,0:T(8,128)(2,1)}, u32[]{:S(2)}) copy-start(bf16[384,3072]{1,0:T(8,128)(2,1)} %refs_2_.7) | copy-start | bytes 7077892
  57.4 1.3 copy-start.2
  61.4 24.5 %collective-permute-start.19 = (bf16[6,128,384]{2,1,0:T(8,128)(2,1)}, bf16[6,128,384]{2,1,0:T(8,128)(2,1)}, u32[]{:S(2)}, u32[]{:S(2)}) collective-permute-start(bf16[6,128,384]{2,1,0:T(8,128)(2,1)} %shard_map.101), channel_id=1, source_target_pairs={{0,8},{8,0},{16,24},{24,16},{32,40},{40,32},{48,56},{56,48},{64,72... | collective-permute-start | bytes 1769480 | tf_op jit(solution)/shard_map/ppermute | solution.py:50
  61.5 12.3 %copy-start.13 = (bf16[384,384]{1,0:T(8,128)(2,1)}, bf16[384,384]{1,0:T(8,128)(2,1)S(1)}, u32[]{:S(2)}) copy-start(bf16[384,384]{1,0:T(8,128)(2,1)S(1)} %collective-permute-done.2.refs_5_) | copy-start | bytes 884740
  61.6 11.2 %collective-permute-start.4 = (bf16[384,384]{1,0:T(8,128)(2,1)S(1)}, bf16[384,384]{1,0:T(8,128)(2,1)S(1)}, u32[]{:S(2)}, u32[]{:S(2)}) collective-permute-start(bf16[384,384]{1,0:T(8,128)(2,1)S(1)} %collective-permute-done.2.refs_5_), channel_id=1, source_target_pairs={{0,1},{1,2},{2,3},{3,4},{4,5},{5,6},{6,7},{7,0},{8,9},{9,10},{10,1... | collective-permute-start | bytes 884744 | tf_op jit(solution)/shard_map/ppermute | solution.py:410
  61.7 13.0 %copy-start.15 = (bf16[384,384]{1,0:T(8,128)(2,1)}, bf16[384,384]{1,0:T(8,128)(2,1)S(1)}, u32[]{:S(2)}) copy-start(bf16[384,384]{1,0:T(8,128)(2,1)S(1)} %collective-permute-done.3.refs_6_) | copy-start | bytes 884740
  61.7 11.1 %collective-permute-start.5 = (bf16[384,384]{1,0:T(8,128)(2,1)S(1)}, bf16[384,384]{1,0:T(8,128)(2,1)S(1)}, u32[]{:S(2)}, u32[]{:S(2)}) collective-permute-start(bf16[384,384]{1,0:T(8,128)(2,1)S(1)} %collective-permute-done.3.refs_6_), channel_id=1, source_target_pairs={{0,7},{1,0},{2,1},{3,2},{4,3},{5,4},{6,5},{7,6},{8,15},{9,8},{10,9... | collective-permute-start | bytes 884744 | tf_op jit(solution)/shard_map/ppermute | solution.py:410
  73.9 0.7 copy-start.4
  74.6 9.4 %collective-permute-start.6 = (bf16[192,384]{1,0:T(8,128)(2,1)}, bf16[192,384]{1,0:T(8,128)(2,1)}, u32[]{:S(2)}, u32[]{:S(2)}) collective-permute-start(bf16[192,384]{1,0:T(8,128)(2,1)} %get-tuple-element.38), channel_id=1, source_target_pairs={{0,1},{1,2},{2,3},{3,4},{4,5},{5,6},{6,7},{7,0},{8,9},{9,10},{10,1... | collective-permute-start | bytes 442376 | tf_op jit(solution)/shard_map/ppermute | solution.py:410
  74.6 9.4 %collective-permute-start.7 = (bf16[192,384]{1,0:T(8,128)(2,1)}, bf16[192,384]{1,0:T(8,128)(2,1)}, u32[]{:S(2)}, u32[]{:S(2)}) collective-permute-start(bf16[192,384]{1,0:T(8,128)(2,1)} %get-tuple-element.39), channel_id=1, source_target_pairs={{0,7},{1,0},{2,1},{3,2},{4,3},{5,4},{6,5},{7,6},{8,15},{9,8},{10,9... | collective-permute-start | bytes 442376 | tf_op jit(solution)/shard_map/ppermute | solution.py:410
  77.9 6.2 %copy-start.5 = (bf16[384,384]{1,0:T(8,128)(2,1)S(1)}, bf16[384,384]{1,0:T(8,128)(2,1)}, u32[]{:S(2)}) copy-start(bf16[384,384]{1,0:T(8,128)(2,1)} %copy-done.4) | copy-start | bytes 884740
  77.9 1.0 copy-start.9
  78.9 1.0 copy-start.12
  79.8 1.0 copy-start.14
  80.8 1.0 copy-start.16
  84.0 1.9 %copy-start.3 = (bf16[8,128,384]{2,1,0:T(8,128)(2,1)S(1)}, bf16[8,128,384]{2,1,0:T(8,128)(2,1)}, u32[]{:S(2)}) copy-start(bf16[8,128,384]{2,1,0:T(8,128)(2,1)} %copy-done.1) | copy-start | bytes 2359300
  84.0 1.9 %copy-start.6 = (bf16[384,384]{1,0:T(8,128)(2,1)S(1)}, bf16[384,384]{1,0:T(8,128)(2,1)}, u32[]{:S(2)}) copy-start(bf16[384,384]{1,0:T(8,128)(2,1)} %refs_3_.3) | copy-start | bytes 884740
  84.0 1.9 %copy-start.7 = (bf16[384,384]{1,0:T(8,128)(2,1)S(1)}, bf16[384,384]{1,0:T(8,128)(2,1)}, u32[]{:S(2)}) copy-start(bf16[384,384]{1,0:T(8,128)(2,1)} %refs_4_.1) | copy-start | bytes 884740
  84.0 1.9 %copy-start.10 = (bf16[384,384]{1,0:T(8,128)(2,1)S(1)}, bf16[384,384]{1,0:T(8,128)(2,1)}, u32[]{:S(2)}) copy-start(bf16[384,384]{1,0:T(8,128)(2,1)} %refs_2_.6) | copy-start | bytes 884740
  93.8 2.1 %collective-permute-start.28 = (bf16[6,128,384]{2,1,0:T(8,128)(2,1)S(1)}, bf16[6,128,384]{2,1,0:T(8,128)(2,1)S(1)}, u32[]{:S(2)}, u32[]{:S(2)}) collective-permute-start(bf16[6,128,384]{2,1,0:T(8,128)(2,1)S(1)} %get-tuple-element.54), channel_id=1, source_target_pairs={{0,8},{8,0},{16,24},{24,16},{32,40},{40,32},{48,56},{56,48},{64,72... | collective-permute-start | bytes 1769480 | tf_op jit(solution)/shard_map/ppermute | solution.py:50
  97.4 17.7 %collective-permute-start.29 = (bf16[8,128,384]{2,1,0:T(8,128)(2,1)S(1)}, bf16[8,128,384]{2,1,0:T(8,128)(2,1)S(1)}, u32[]{:S(2)}, u32[]{:S(2)}) collective-permute-start(bf16[8,128,384]{2,1,0:T(8,128)(2,1)S(1)} %get-tuple-element.55), channel_id=1, source_target_pairs={{0,16},{8,72},{16,32},{24,88},{32,48},{40,104},{48,0},{56,120},{64... | collective-permute-start | bytes 2359304 | tf_op jit(solution)/shard_map/ppermute | solution.py:46
  99.6 15.6 %collective-permute-start.30 = (bf16[8,128,384]{2,1,0:T(8,128)(2,1)S(1)}, bf16[8,128,384]{2,1,0:T(8,128)(2,1)S(1)}, u32[]{:S(2)}, u32[]{:S(2)}) collective-permute-start(bf16[8,128,384]{2,1,0:T(8,128)(2,1)S(1)} %get-tuple-element.56), channel_id=1, source_target_pairs={{0,48},{8,200},{16,0},{24,216},{32,16},{40,232},{48,32},{56,248},{... | collective-permute-start | bytes 2359304 | tf_op jit(solution)/shard_map/ppermute | solution.py:46
  103.4 5.2 %collective-permute-start.24 = (bf16[192,384]{1,0:T(8,128)(2,1)S(1)}, bf16[192,384]{1,0:T(8,128)(2,1)S(1)}, u32[]{:S(2)}, u32[]{:S(2)}) collective-permute-start(bf16[192,384]{1,0:T(8,128)(2,1)S(1)} %get-tuple-element.73), channel_id=1, source_target_pairs={{0,7},{1,0},{2,1},{3,2},{4,3},{5,4},{6,5},{7,6},{8,15},{9,8},{10,9... | collective-permute-start | bytes 442376 | tf_op jit(solution)/shard_map/ppermute | solution.py:410
  105.2 12.1 %collective-permute-start.20 = (bf16[192,384]{1,0:T(8,128)(2,1)S(1)}, bf16[192,384]{1,0:T(8,128)(2,1)S(1)}, u32[]{:S(2)}, u32[]{:S(2)}) collective-permute-start(bf16[192,384]{1,0:T(8,128)(2,1)S(1)} %get-tuple-element.72), channel_id=1, source_target_pairs={{0,1},{1,2},{2,3},{3,4},{4,5},{5,6},{6,7},{7,0},{8,9},{9,10},{10,1... | collective-permute-start | bytes 442376 | tf_op jit(solution)/shard_map/ppermute | solution.py:410
  108.7 10.0 %collective-permute-start.25 = (bf16[384,384]{1,0:T(8,128)(2,1)S(1)}, bf16[384,384]{1,0:T(8,128)(2,1)S(1)}, u32[]{:S(2)}, u32[]{:S(2)}) collective-permute-start(bf16[384,384]{1,0:T(8,128)(2,1)S(1)} %pad_maximum_fusion.1), channel_id=1, source_target_pairs={{0,7},{1,0},{2,1},{3,2},{4,3},{5,4},{6,5},{7,6},{8,15},{9,8},{10,9... | collective-permute-start | bytes 884744 | tf_op jit(solution)/shard_map/ppermute | solution.py:410
  111.9 15.5 %collective-permute-start.32 = (bf16[8,128,384]{2,1,0:T(8,128)(2,1)S(1)}, bf16[8,128,384]{2,1,0:T(8,128)(2,1)S(1)}, u32[]{:S(2)}, u32[]{:S(2)}) collective-permute-start(bf16[8,128,384]{2,1,0:T(8,128)(2,1)S(1)} %get-tuple-element.58), channel_id=1, source_target_pairs={{0,48},{8,200},{16,0},{24,216},{32,16},{40,232},{48,32},{56,248},{... | collective-permute-start | bytes 2359304 | tf_op jit(solution)/shard_map/ppermute | solution.py:46
  115.2 13.7 %collective-permute-start.33 = (bf16[8,128,384]{2,1,0:T(8,128)(2,1)S(1)}, bf16[8,128,384]{2,1,0:T(8,128)(2,1)S(1)}, u32[]{:S(2)}, u32[]{:S(2)}) collective-permute-start(bf16[8,128,384]{2,1,0:T(8,128)(2,1)S(1)} %get-tuple-element.59), channel_id=1, source_target_pairs={{0,16},{8,72},{16,32},{24,88},{32,48},{40,104},{48,0},{56,120},{64... | collective-permute-start | bytes 2359304 | tf_op jit(solution)/shard_map/ppermute | solution.py:46
  116.4 19.2 %collective-permute-start.31 = (bf16[8,128,384]{2,1,0:T(8,128)(2,1)S(1)}, bf16[8,128,384]{2,1,0:T(8,128)(2,1)S(1)}, u32[]{:S(2)}, u32[]{:S(2)}) collective-permute-start(bf16[8,128,384]{2,1,0:T(8,128)(2,1)S(1)} %get-tuple-element.57), channel_id=1, source_target_pairs={{0,16},{8,72},{16,32},{24,88},{32,48},{40,104},{48,0},{56,120},{64... | collective-permute-start | bytes 2359304 | tf_op jit(solution)/shard_map/ppermute | solution.py:46
  117.3 18.2 %collective-permute-start.34 = (bf16[8,128,384]{2,1,0:T(8,128)(2,1)S(1)}, bf16[8,128,384]{2,1,0:T(8,128)(2,1)S(1)}, u32[]{:S(2)}, u32[]{:S(2)}) collective-permute-start(bf16[8,128,384]{2,1,0:T(8,128)(2,1)S(1)} %get-tuple-element.60), channel_id=1, source_target_pairs={{0,48},{8,200},{16,0},{24,216},{32,16},{40,232},{48,32},{56,248},{... | collective-permute-start | bytes 2359304 | tf_op jit(solution)/shard_map/ppermute | solution.py:46
  118.7 8.0 %collective-permute-start.21 = (bf16[384,384]{1,0:T(8,128)(2,1)S(1)}, bf16[384,384]{1,0:T(8,128)(2,1)S(1)}, u32[]{:S(2)}, u32[]{:S(2)}) collective-permute-start(bf16[384,384]{1,0:T(8,128)(2,1)S(1)} %pad_maximum_fusion), channel_id=1, source_target_pairs={{0,1},{1,2},{2,3},{3,4},{4,5},{5,6},{6,7},{7,0},{8,9},{9,10},{10,1... | collective-permute-start | bytes 884744 | tf_op jit(solution)/shard_map/ppermute | solution.py:410
  126.7 13.7 %collective-permute-start.26 = (bf16[384,384]{1,0:T(8,128)(2,1)S(1)}, bf16[384,384]{1,0:T(8,128)(2,1)S(1)}, u32[]{:S(2)}, u32[]{:S(2)}) collective-permute-start(bf16[384,384]{1,0:T(8,128)(2,1)S(1)} %add_convert_fusion.2), channel_id=1, source_target_pairs={{0,7},{1,0},{2,1},{3,2},{4,3},{5,4},{6,5},{7,6},{8,15},{9,8},{10,9... | collective-permute-start | bytes 884744 | tf_op jit(solution)/shard_map/ppermute | solution.py:410
  127.4 20.2 %collective-permute-start.22 = (bf16[384,384]{1,0:T(8,128)(2,1)S(1)}, bf16[384,384]{1,0:T(8,128)(2,1)S(1)}, u32[]{:S(2)}, u32[]{:S(2)}) collective-permute-start(bf16[384,384]{1,0:T(8,128)(2,1)S(1)} %add_convert_fusion.4), channel_id=1, source_target_pairs={{0,1},{1,2},{2,3},{3,4},{4,5},{5,6},{6,7},{7,0},{8,9},{9,10},{10,1... | collective-permute-start | bytes 884744 | tf_op jit(solution)/shard_map/ppermute | solution.py:410
  137.1 7.0 %collective-permute-start.35 = (bf16[2,128,384]{2,1,0:T(8,128)(2,1)S(1)}, bf16[2,128,384]{2,1,0:T(8,128)(2,1)S(1)}, u32[]{:S(2)}, u32[]{:S(2)}) collective-permute-start(bf16[2,128,384]{2,1,0:T(8,128)(2,1)S(1)} %get-tuple-element.64), channel_id=1, source_target_pairs={{0,64},{8,24},{16,80},{24,40},{32,96},{40,56},{48,112},{56,8},{64,... | collective-permute-start | bytes 589832 | tf_op jit(solution)/shard_map/ppermute | solution.py:46
  137.2 6.9 %collective-permute-start.36 = (bf16[2,128,384]{2,1,0:T(8,128)(2,1)S(1)}, bf16[2,128,384]{2,1,0:T(8,128)(2,1)S(1)}, u32[]{:S(2)}, u32[]{:S(2)}) collective-permute-start(bf16[2,128,384]{2,1,0:T(8,128)(2,1)S(1)} %get-tuple-element.65), channel_id=1, source_target_pairs={{0,192},{8,56},{16,208},{24,8},{32,224},{40,24},{48,240},{56,40},{... | collective-permute-start | bytes 589832 | tf_op jit(solution)/shard_map/ppermute | solution.py:46
  140.5 13.0 %collective-permute-start.27 = (bf16[384,384]{1,0:T(8,128)(2,1)S(1)}, bf16[384,384]{1,0:T(8,128)(2,1)S(1)}, u32[]{:S(2)}, u32[]{:S(2)}) collective-permute-start(bf16[384,384]{1,0:T(8,128)(2,1)S(1)} %add_convert_fusion.1), channel_id=1, source_target_pairs={{0,7},{1,0},{2,1},{3,2},{4,3},{5,4},{6,5},{7,6},{8,15},{9,8},{10,9... | collective-permute-start | bytes 884744 | tf_op jit(solution)/shard_map/ppermute | solution.py:410
  144.2 9.1 %collective-permute-start.37 = (bf16[4,128,384]{2,1,0:T(8,128)(2,1)S(1)}, bf16[4,128,384]{2,1,0:T(8,128)(2,1)S(1)}, u32[]{:S(2)}, u32[]{:S(2)}) collective-permute-start(bf16[4,128,384]{2,1,0:T(8,128)(2,1)S(1)} %get-tuple-element.66), channel_id=1, source_target_pairs={{0,64},{8,24},{16,80},{24,40},{32,96},{40,56},{48,112},{56,8},{64,... | collective-permute-start | bytes 1179656 | tf_op jit(solution)/shard_map/ppermute | solution.py:46
  144.2 9.0 %collective-permute-start.38 = (bf16[4,128,384]{2,1,0:T(8,128)(2,1)S(1)}, bf16[4,128,384]{2,1,0:T(8,128)(2,1)S(1)}, u32[]{:S(2)}, u32[]{:S(2)}) collective-permute-start(bf16[4,128,384]{2,1,0:T(8,128)(2,1)S(1)} %get-tuple-element.67), channel_id=1, source_target_pairs={{0,192},{8,56},{16,208},{24,8},{32,224},{40,24},{48,240},{56,40},{... | collective-permute-start | bytes 1179656 | tf_op jit(solution)/shard_map/ppermute | solution.py:46
  147.6 8.0 %collective-permute-start.23 = (bf16[384,384]{1,0:T(8,128)(2,1)S(1)}, bf16[384,384]{1,0:T(8,128)(2,1)S(1)}, u32[]{:S(2)}, u32[]{:S(2)}) collective-permute-start(bf16[384,384]{1,0:T(8,128)(2,1)S(1)} %add_convert_fusion.3), channel_id=1, source_target_pairs={{0,1},{1,2},{2,3},{3,4},{4,5},{5,6},{6,7},{7,0},{8,9},{9,10},{10,1... | collective-permute-start | bytes 884744 | tf_op jit(solution)/shard_map/ppermute | solution.py:410
  153.4 3.1 %collective-permute-start.39 = (bf16[2,128,384]{2,1,0:T(8,128)(2,1)S(1)}, bf16[2,128,384]{2,1,0:T(8,128)(2,1)S(1)}, u32[]{:S(2)}, u32[]{:S(2)}) collective-permute-start(bf16[2,128,384]{2,1,0:T(8,128)(2,1)S(1)} %get-tuple-element.69), channel_id=1, source_target_pairs={{0,8},{8,0},{16,24},{24,16},{32,40},{40,32},{48,56},{56,48},{64,72... | collective-permute-start | bytes 589832 | tf_op jit(solution)/shard_map/ppermute | solution.py:50
where the time goes:
time: 160 us; the launch traced here: 158 us
  waiting for transfers between devices  63.1 us (39%)
  starting transfers between devices  55.4 us (35%)
  Pallas kernels  28.4 us (18%)
  local copies, waits for them, and re-layouts  8.53 us (5%)
    ppermute x20, waiting for transfers between devices, hop(): return lax.ppermute(x, 'seq', steps_of(leg, sign))  34.5 us
    ppermute x20, starting transfers between devices, hop(): return lax.ppermute(x, 'seq', steps_of(leg, sign))  29.3 us
    pallas_call x17, Pallas kernels, call(): pl.pallas_call(body, in_specs=in_specs, out_specs=out_specs or [VMEM] * l...  28.4 us
    ppermute x16, starting transfers between devices, ring_pair(): lax.ppermute(x, 'head', [(i, (i + sign) % size) for i in range(size)])  25.7 us
    ppermute x16, waiting for transfers between devices, ring_pair(): lax.ppermute(x, 'head', [(i, (i + sign) % size) for i in range(size)])  25.2 us
    unnamed x39, local copies, waits for them, and re-layouts  8.32 us
    ppermute x4, waiting for transfers between devices, swap(): return lax.ppermute(x, 'seq', swap_of())  3.42 us
  transfers between devices with their start and end apart: 40, of which 15 were waited for; matrix products, arithmetic and copies ran while one was open for 1% of the time, Pallas kernels for 10%

commit v1 on v0

--- a/solution.py
+++ b/solution.py
@@ -245,11 +245,11 @@
         def body(number, carry):
             code = table[group * far_count + number]
             first = table[(2 + group) * far_count + number] != 0
-            for kind, ref in cases:
-
-                @pl.when(first & (code // 16 == kind))
+            for kind, low, high, ref in cases:
+
+                @pl.when(first & (code >= kind * 16 + low) & (code < kind * 16 + high))
                 def _():
-                    index = code % 16
+                    index = code - (kind * 16 + low)
 
                     @pl.loop(0, 4)
                     def _(part):
@@ -263,13 +263,13 @@
         lax.fori_loop(0, far_count, body, 0)
 
 
-def early_body(table, mine, theirs, far_low, far_high, up, down):
+def pair_body(first_kind, second_kind, table, mine, theirs, first, second):
     @pl.loop(0, 8)
     def _(index):
-        for ref in (far_low, far_high, up, down):
+        for ref in (first, second):
             ref[index] = jnp.zeros(ref.shape[1:], ref.dtype)
 
-    add_terms(table, mine, theirs, ((3, far_low), (7, far_high), (6, up), (1, down)))
+    add_terms(table, mine, theirs, ((first_kind, 0, 8, first), (second_kind, 0, 8, second)))
 
 
 def late_body(table, mine, theirs, from_low, from_high, up, down):
@@ -278,28 +278,38 @@
         up[index] = from_low[index]
         down[index] = from_high[index]
 
-    add_terms(table, mine, theirs, ((2, up), (5, down)))
-
-
-def mid_body(table, mine, theirs, low_first, high_first, low_second, high_second, own, down, up, far_low, far_high, first, second):
+    add_terms(table, mine, theirs, ((2, 0, 8, up), (5, 0, 8, down)))
+
+
+def opposite_body(table, mine, theirs, low_second, high_second, far_low, far_high, total):
     f32, bf16 = jnp.float32, jnp.bfloat16
 
-    @pl.loop(0, 8)
+    @pl.loop(0, 4)
+    def _(index):
+        total[index] = low_second[index + 4].astype(f32) + high_second[index + 4].astype(f32)
+
+    add_terms(table, mine, theirs, ((4, 4, 8, total),))
+    for index in range(2):
+        far_low[index] = total[index].astype(bf16)
+        far_high[index] = total[index + 2].astype(bf16)
+
+
+def mid_body(table, mine, theirs, low_first, high_first, low_second, high_second, own, down, up, first, second):
+    f32, bf16 = jnp.float32, jnp.bfloat16
+
+    @pl.loop(0, 4)
     def _(index):
         first[index] = low_first[index].astype(f32) + high_first[index].astype(f32)
+        first[index + 4] = low_first[index + 4].astype(f32) + high_first[index + 4].astype(f32)
         second[index] = low_second[index].astype(f32) + high_second[index].astype(f32)
 
-    add_terms(table, mine, theirs, ((0, first), (4, second)))
+    add_terms(table, mine, theirs, ((0, 0, 8, first), (4, 0, 4, second)))
 
     @pl.loop(0, 4)
     def _(index):
         own[index] = first[index].astype(bf16)
         down[index] = first[index + 4].astype(bf16)
         up[index] = second[index].astype(bf16)
-
-    for index in range(2):
-        far_low[index] = second[index + 4].astype(bf16)
-        far_high[index] = second[index + 6].astype(bf16)
 
 
 def turn_body(down, up, from_low, from_high, down_out, up_out):
@@ -519,7 +529,8 @@
     lead = (table, terms, theirs)
     lead_specs = [SMEM, VMEM, VMEM]
     eight = shape(8, BLK, width)
-    far_low, far_high, up_b, down_a = call(early_body, lead_specs, [eight] * 4, *lead)
+    far_low, far_high = call(lambda *refs: pair_body(3, 7, *refs), lead_specs, [eight] * 2, *lead)
+    up_b, down_a = call(lambda *refs: pair_body(6, 1, *refs), lead_specs, [eight] * 2, *lead)
     from_low, from_high = hop(far_low, 1, 1), hop(far_high, 1, -1)
     low_b, high_a = hop(up_b, 1, 1), hop(down_a, 1, -1)
     ahead, back = ring_pair((parts[half][:cut], parts[half][cut:]))
@@ -532,10 +543,14 @@
         if distance:
             ahead, back = add(parts[distance], ahead), add(parts[size - distance], back)
     attended = add(parts[0], ahead, back)
-    own, down, up, far_low, far_high = call(
-        mid_body, lead_specs + [VMEM] * 4, [shape(4, BLK, width)] * 3 + [piece] * 2,
+    far_low, far_high = call(
+        opposite_body, lead_specs + [VMEM] * 2, [piece] * 2, *lead, low_b, high_b,
+        scratch=[pltpu.VMEM((4, BLK, width), f32)],
+    )
+    own, down, up = call(
+        mid_body, lead_specs + [VMEM] * 4, [shape(4, BLK, width)] * 3,
         *lead, low_a, high_a, low_b, high_b,
-        scratch=[pltpu.VMEM((8, BLK, width), f32)] * 2,
+        scratch=[pltpu.VMEM((8, BLK, width), f32), pltpu.VMEM((4, BLK, width), f32)],
     )
     down, up = call(
         turn_body, [VMEM] * 4, [shape(4, BLK, width)] * 2,

time: 160 us -> 156 us (0.975)
  waiting for transfers between devices: 63.1 us -> 58 us
    ppermute x20, waiting for transfers between devices: 34.5 us -> 29.2 us  [hop(): return lax.ppermute(x, 'seq', steps_of(leg, sign))]
    ppermute x20, starting transfers between devices: 29.3 us -> 27.4 us  [hop(): return lax.ppermute(x, 'seq', steps_of(leg, sign))]
    pallas_call x17 -> x19, Pallas kernels: 28.4 us -> 29.7 us  [call(): pl.pallas_call(body, in_specs=in_specs, out_specs=out_specs or [VMEM] * l...]
  transfers between devices with their start and end apart: 40 -> 40, of which waited for: 15 -> 17; matrix products, arithmetic and copies ran while one was open for 1% -> 1% of each run, Pallas kernels for 10% -> 12%
where the time goes in v1:
time: 156 us; the launch traced here: 154 us
  waiting for transfers between devices  58 us (37%)
  starting transfers between devices  54.9 us (35%)
  Pallas kernels  29.7 us (19%)
  local copies, waits for them, and re-layouts  8.52 us (5%)
    pallas_call x19, Pallas kernels, call(): pl.pallas_call(body, in_specs=in_specs, out_specs=out_specs or [VMEM] * l...  29.7 us
    ppermute x20, waiting for transfers between devices, hop(): return lax.ppermute(x, 'seq', steps_of(leg, sign))  29.2 us
    ppermute x20, starting transfers between devices, hop(): return lax.ppermute(x, 'seq', steps_of(leg, sign))  27.4 us
    ppermute x16, starting transfers between devices, ring_pair(): lax.ppermute(x, 'head', [(i, (i + sign) % size) for i in range(size)])  27.1 us
    ppermute x16, waiting for transfers between devices, ring_pair(): lax.ppermute(x, 'head', [(i, (i + sign) % size) for i in range(size)])  25.4 us
    unnamed x39, local copies, waits for them, and re-layouts  8.31 us
    ppermute x4, waiting for transfers between devices, swap(): return lax.ppermute(x, 'seq', swap_of())  3.42 us
  transfers between devices with their start and end apart: 40, of which 17 were waited for; matrix products, arithmetic and copies ran while one was open for 1% of the time, Pallas kernels for 12%

profile of v1, /device:TPU:8, one launch (start us, length us, event | category | flops | bytes accessed | tf_op | source)
XLA Modules:
  0.0 153.8 jit_solution(3686492498929312988)
XLA Ops:
  0.6 0.7 copy-done.17
  1.3 1.2 shard_map.97
  2.6 1.4 collective-permute-done.8.refs_1_
  4.1 2.8 %collective-permute-start.13 = (bf16[4,128,384]{2,1,0:T(8,128)(2,1)S(1)}, bf16[4,128,384]{2,1,0:T(8,128)(2,1)S(1)}, u32[]{:S(2)}, u32[]{:S(2)}) collective-permute-start(bf16[4,128,384]{2,1,0:T(8,128)(2,1)S(1)} %shard_map.98.refs_0_), channel_id=1, source_target_pairs={{0,192},{8,56},{16,208},{24,8},{32,224},{40,24},{48,240},{56,40},{... | collective-permute-start | bytes 1179656 | tf_op jit(solution)/shard_map/ppermute | solution.py:46
  6.9 5.3 %collective-permute-done.13.refs_0_ = bf16[4,128,384]{2,1,0:T(8,128)(2,1)S(1)} collective-permute-done((bf16[4,128,384]{2,1,0:T(8,128)(2,1)S(1)}, bf16[4,128,384]{2,1,0:T(8,128)(2,1)S(1)}, u32[]{:S(2)}, u32[]{:S(2)}) %collective-permute-start.13) | collective-permute-done | bytes 393248 | tf_op jit(solution)/shard_map/ppermute | solution.py:46
  12.3 3.8 %collective-permute-start.15 = (bf16[2,128,384]{2,1,0:T(8,128)(2,1)S(1)}, bf16[2,128,384]{2,1,0:T(8,128)(2,1)S(1)}, u32[]{:S(2)}, u32[]{:S(2)}) collective-permute-start(bf16[2,128,384]{2,1,0:T(8,128)(2,1)S(1)} %slice.41), channel_id=1, source_target_pairs={{0,192},{8,56},{16,208},{24,8},{32,224},{40,24},{48,240},{56,40},{... | collective-permute-start | bytes 589832 | tf_op jit(solution)/shard_map/ppermute | solution.py:46
  16.2 1.7 %collective-permute-start.10 = (bf16[8,128,384]{2,1,0:T(8,128)(2,1)S(1)}, bf16[8,128,384]{2,1,0:T(8,128)(2,1)}, u32[]{:S(2)}, u32[]{:S(2)}) collective-permute-start(bf16[8,128,384]{2,1,0:T(8,128)(2,1)S(1)} %shard_map.99.refs_1_.refs_7_), channel_id=1, source_target_pairs={{0,16},{8,72},{16,32},{24,88},{32,48},{40,104},{48,0},{56,120},{64... | collective-permute-start | bytes 2359304 | tf_op jit(solution)/shard_map/ppermute | solution.py:46
  17.9 1.3 collective-permute-done.15.refs_2_
  19.2 5.9 %collective-permute-done.14.refs_1_ = bf16[2,128,384]{2,1,0:T(8,128)(2,1)S(1)} collective-permute-done((bf16[2,128,384]{2,1,0:T(8,128)(2,1)S(1)}, bf16[2,128,384]{2,1,0:T(8,128)(2,1)S(1)}, u32[]{:S(2)}, u32[]{:S(2)}) %collective-permute-start.14) | collective-permute-done | bytes 196640 | tf_op jit(solution)/shard_map/ppermute | solution.py:46
  25.1 1.0 shard_map.100.refs_5_.refs_11_
  26.1 0.5 collective-permute-start.17
  26.5 3.0 %collective-permute-start.11 = (bf16[8,128,384]{2,1,0:T(8,128)(2,1)S(1)}, bf16[8,128,384]{2,1,0:T(8,128)(2,1)S(1)}, u32[]{:S(2)}, u32[]{:S(2)}) collective-permute-start(bf16[8,128,384]{2,1,0:T(8,128)(2,1)S(1)} %shard_map.99.refs_1_.refs_7_), channel_id=1, source_target_pairs={{0,48},{8,200},{16,0},{24,216},{32,16},{40,232},{48,32},{56,248},{... | collective-permute-start | bytes 2359304 | tf_op jit(solution)/shard_map/ppermute | solution.py:46
  29.5 1.9 %collective-permute-start = (bf16[384,384]{1,0:T(8,128)(2,1)S(1)}, bf16[384,384]{1,0:T(8,128)(2,1)S(1)}, u32[]{:S(2)}, u32[]{:S(2)}) collective-permute-start(bf16[384,384]{1,0:T(8,128)(2,1)S(1)} %copy-done.8), channel_id=1, source_target_pairs={{0,1},{1,2},{2,3},{3,4},{4,5},{5,6},{6,7},{7,0},{8,9},{9,10},{10,1... | collective-permute-start | bytes 884744 | tf_op jit(solution)/shard_map/ppermute | solution.py:420
  31.5 0.6 collective-permute-start.12
  32.0 6.3 %collective-permute-done.17.refs_7_.refs_13_ = bf16[8,128,384]{2,1,0:T(8,128)(2,1)} collective-permute-done((bf16[8,128,384]{2,1,0:T(8,128)(2,1)}, bf16[8,128,384]{2,1,0:T(8,128)(2,1)}, u32[]{:S(2)}, u32[]{:S(2)}) %collective-permute-start.17) | collective-permute-done | bytes 786464 | tf_op jit(solution)/shard_map/ppermute | solution.py:46
  38.4 1.0 collective-permute-start.18
  39.4 0.7 collective-permute-done.refs_3_
  40.1 5.1 %collective-permute-start.1 = (bf16[384,384]{1,0:T(8,128)(2,1)S(1)}, bf16[384,384]{1,0:T(8,128)(2,1)}, u32[]{:S(2)}, u32[]{:S(2)}) collective-permute-start(bf16[384,384]{1,0:T(8,128)(2,1)S(1)} %copy-done.8), channel_id=1, source_target_pairs={{0,7},{1,0},{2,1},{3,2},{4,3},{5,4},{6,5},{7,6},{8,15},{9,8},{10,9... | collective-permute-start | bytes 884744 | tf_op jit(solution)/shard_map/ppermute | solution.py:420
  45.5 4.0 %collective-permute-done.1.refs_4_ = bf16[384,384]{1,0:T(8,128)(2,1)} collective-permute-done((bf16[384,384]{1,0:T(8,128)(2,1)S(1)}, bf16[384,384]{1,0:T(8,128)(2,1)}, u32[]{:S(2)}, u32[]{:S(2)}) %collective-permute-start.1) | collective-permute-done | bytes 294944 | tf_op jit(solution)/shard_map/ppermute | solution.py:420
  49.5 0.7 copy-done.11
  50.2 0.9 copy-done.1
  51.1 3.9 %collective-permute-start.3 = (bf16[384,384]{1,0:T(8,128)(2,1)}, bf16[384,384]{1,0:T(8,128)(2,1)S(1)}, u32[]{:S(2)}, u32[]{:S(2)}) collective-permute-start(bf16[384,384]{1,0:T(8,128)(2,1)} %collective-permute-done.1.refs_4_), channel_id=1, source_target_pairs={{0,7},{1,0},{2,1},{3,2},{4,3},{5,4},{6,5},{7,6},{8,15},{9,8},{10,9... | collective-permute-start | bytes 884744 | tf_op jit(solution)/shard_map/ppermute | solution.py:420
  55.1 2.2 %shard_map.93.refs_0_.table = s32[49]{0:T(128)S(1)} custom-call(s32[4,96]{1,0:T(4,128)S(1)} %bitcast.6, s32[96]{0:T(128)S(1)} %compare_select_fusion.1.refs_1_.refs_0_, s32[1]{0:T(128)} %bitcast.2.refs_2_.refs_1_), custom_call_target="tpu_custom_call" | custom-call | tf_op jit(solution)/shard_map/pallas_call | solution.py:438
  57.4 1.3 copy-done.2
  58.7 2.8 %shard_map.101 = bf16[6,128,384]{2,1,0:T(8,128)(2,1)} custom-call(s32[49]{0:T(128)S(1)} %shard_map.93.refs_0_.table, bf16[8,128,384]{2,1,0:T(8,128)(2,1)S(1)} %shard_map.99.refs_1_.refs_7_, bf16[8,128,384]{2,1,0:T(8,128)(2,1)} %collective-permute-done.10.refs_2_.refs_8_, bf16[8,128,384]{2,1,0:T(8,128)(2,1)S(1)} %copy-done.2, ...), custom_call_target="tpu_custom_call" | custom-call | tf_op jit(solution)/shard_map/pallas_call | solution.py:438
  61.7 3.6 %collective-permute-start.5 = (bf16[384,384]{1,0:T(8,128)(2,1)S(1)}, bf16[384,384]{1,0:T(8,128)(2,1)S(1)}, u32[]{:S(2)}, u32[]{:S(2)}) collective-permute-start(bf16[384,384]{1,0:T(8,128)(2,1)S(1)} %collective-permute-done.3.refs_6_), channel_id=1, source_target_pairs={{0,7},{1,0},{2,1},{3,2},{4,3},{5,4},{6,5},{7,6},{8,15},{9,8},{10,9... | collective-permute-start | bytes 884744 | tf_op jit(solution)/shard_map/ppermute | solution.py:420
  65.3 7.5 %collective-permute-done.4.low.refs_3_ = bf16[384,384]{1,0:T(8,128)(2,1)S(1)} collective-permute-done((bf16[384,384]{1,0:T(8,128)(2,1)S(1)}, bf16[384,384]{1,0:T(8,128)(2,1)S(1)}, u32[]{:S(2)}, u32[]{:S(2)}) %collective-permute-start.4) | collective-permute-done | bytes 294944 | tf_op jit(solution)/shard_map/ppermute | solution.py:420
  72.8 1.1 shard_map.95
  73.9 0.7 copy-done.4
  74.6 3.2 %collective-permute-start.7 = (bf16[192,384]{1,0:T(8,128)(2,1)}, bf16[192,384]{1,0:T(8,128)(2,1)}, u32[]{:S(2)}, u32[]{:S(2)}) collective-permute-start(bf16[192,384]{1,0:T(8,128)(2,1)} %get-tuple-element.39), channel_id=1, source_target_pairs={{0,7},{1,0},{2,1},{3,2},{4,3},{5,4},{6,5},{7,6},{8,15},{9,8},{10,9... | collective-permute-start | bytes 442376 | tf_op jit(solution)/shard_map/ppermute | solution.py:420
  77.9 1.0 copy-done.9
  78.9 1.0 copy-done.12
  79.9 1.0 copy-done.14
  80.8 1.0 copy-done.16
  81.8 2.2 %shard_map.94.refs_2_ = f32[384,384]{1,0:T(8,128)S(1)} custom-call(s32[1]{0:T(128)} %bitcast.refs_0_, bf16[384,3072]{1,0:T(8,128)(2,1)S(1)} %copy-done, bf16[384,384]{1,0:T(8,128)(2,1)S(1)} %copy-done.9, bf16[384,384]{1,0:T(8,128)(2,1)S(1)} %copy-done.12, bf16[384,384]{1,0:T(8,128)(2,1)} %collective-permute-done.1.refs_4_, bf16[384,384]{1,0:T(8,128)(2,1)S(1)} %copy-done.14, ...), custom_call_target="tpu_custom_call" | custom-call | tf_op jit(solution)/shard_map/pallas_call | solution.py:438
  84.1 1.8 %shard_map.96.refs_5_ = bf16[384,384]{1,0:T(8,128)(2,1)S(1)} custom-call(s32[1]{0:T(128)} %bitcast.refs_0_, bf16[384,3072]{1,0:T(8,128)(2,1)S(1)} %copy-done, f32[384,384]{1,0:T(8,128)S(1)} %shard_map.94.refs_2_, bf16[384,384]{1,0:T(8,128)(2,1)S(1)} %collective-permute-done.4.low.refs_3_, bf16[384,384]{1,0:T(8,128)(2,1)S(1)} %copy-done.5, ...), custom_call_target="tpu_custom_call" | custom-call | tf_op jit(solution)/shard_map/pallas_call | solution.py:438
  86.0 7.8 %shard_map.102 = (bf16[384,384]{1,0:T(8,128)(2,1)S(1)}, bf16[384,384]{1,0:T(8,128)(2,1)}, f32[2,384,384]{2,1,0:T(8,128)S(1)}, bf16[6,128,384]{2,1,0:T(8,128)(2,1)S(1)}, bf16[6,128,384]{2,1,0:T(8,128)(2,1)S(1)}) custom-call(s32[49]{0:T(128)S(1)} %shard_map.93.refs_0_.table, s32[1]{0:T(128)} %bitcast.2.refs_2_.refs_1_, bf16[384,384]{1,0:T(8,128)(2,1)S(1)} %copy-done.10, ...), custom_call_target="tpu_custom_call" | custom-call | tf_op jit(solution)/shard_map/pallas_call | solution.py:438
  93.9 2.0 %collective-permute-done.28.refs_2_.theirs = bf16[6,128,384]{2,1,0:T(8,128)(2,1)S(1)} collective-permute-done((bf16[6,128,384]{2,1,0:T(8,128)(2,1)S(1)}, bf16[6,128,384]{2,1,0:T(8,128)(2,1)S(1)}, u32[]{:S(2)}, u32[]{:S(2)}) %collective-permute-start.28) | collective-permute-done | bytes 589856 | tf_op jit(solution)/shard_map/ppermute | solution.py:50
  95.9 1.1 shard_map.104
  97.0 2.2 %collective-permute-start.29 = (bf16[8,128,384]{2,1,0:T(8,128)(2,1)S(1)}, bf16[8,128,384]{2,1,0:T(8,128)(2,1)S(1)}, u32[]{:S(2)}, u32[]{:S(2)}) collective-permute-start(bf16[8,128,384]{2,1,0:T(8,128)(2,1)S(1)} %get-tuple-element.55), channel_id=1, source_target_pairs={{0,16},{8,72},{16,32},{24,88},{32,48},{40,104},{48,0},{56,120},{64... | collective-permute-start | bytes 2359304 | tf_op jit(solution)/shard_map/ppermute | solution.py:46
  99.2 1.7 %collective-permute-start.30 = (bf16[8,128,384]{2,1,0:T(8,128)(2,1)S(1)}, bf16[8,128,384]{2,1,0:T(8,128)(2,1)S(1)}, u32[]{:S(2)}, u32[]{:S(2)}) collective-permute-start(bf16[8,128,384]{2,1,0:T(8,128)(2,1)S(1)} %get-tuple-element.56), channel_id=1, source_target_pairs={{0,48},{8,200},{16,0},{24,216},{32,16},{40,232},{48,32},{56,248},{... | collective-permute-start | bytes 2359304 | tf_op jit(solution)/shard_map/ppermute | solution.py:46
  100.8 2.1 %shard_map.103 = (bf16[384,384]{1,0:T(8,128)(2,1)S(1)}, bf16[384,384]{1,0:T(8,128)(2,1)S(1)}, bf16[384,384]{1,0:T(8,128)(2,1)S(1)}, bf16[384,384]{1,0:T(8,128)(2...) custom-call(s32[1]{0:T(128)} %bitcast.refs_0_, ...), custom_call_target="tpu_custom_call" | custom-call | tf_op jit(solution)/shard_map/pallas_call | solution.py:438
  103.0 1.8 %collective-permute-start.24 = (bf16[192,384]{1,0:T(8,128)(2,1)S(1)}, bf16[192,384]{1,0:T(8,128)(2,1)S(1)}, u32[]{:S(2)}, u32[]{:S(2)}) collective-permute-start(bf16[192,384]{1,0:T(8,128)(2,1)S(1)} %get-tuple-element.73), channel_id=1, source_target_pairs={{0,7},{1,0},{2,1},{3,2},{4,3},{5,4},{6,5},{7,6},{8,15},{9,8},{10,9... | collective-permute-start | bytes 442376 | tf_op jit(solution)/shard_map/ppermute | solution.py:420
  105.2 3.0 %collective-permute-done.24 = bf16[192,384]{1,0:T(8,128)(2,1)S(1)} collective-permute-done((bf16[192,384]{1,0:T(8,128)(2,1)S(1)}, bf16[192,384]{1,0:T(8,128)(2,1)S(1)}, u32[]{:S(2)}, u32[]{:S(2)}) %collective-permute-start.24) | collective-permute-done | bytes 147488 | tf_op jit(solution)/shard_map/ppermute | solution.py:420
  108.3 3.2 %collective-permute-start.25 = (bf16[384,384]{1,0:T(8,128)(2,1)S(1)}, bf16[384,384]{1,0:T(8,128)(2,1)S(1)}, u32[]{:S(2)}, u32[]{:S(2)}) collective-permute-start(bf16[384,384]{1,0:T(8,128)(2,1)S(1)} %pad_maximum_fusion.1), channel_id=1, source_target_pairs={{0,7},{1,0},{2,1},{3,2},{4,3},{5,4},{6,5},{7,6},{8,15},{9,8},{10,9... | collective-permute-start | bytes 884744 | tf_op jit(solution)/shard_map/ppermute | solution.py:420
  111.5 1.1 shard_map.106
  112.6 1.8 %collective-permute-start.33 = (bf16[8,128,384]{2,1,0:T(8,128)(2,1)S(1)}, bf16[8,128,384]{2,1,0:T(8,128)(2,1)S(1)}, u32[]{:S(2)}, u32[]{:S(2)}) collective-permute-start(bf16[8,128,384]{2,1,0:T(8,128)(2,1)S(1)} %get-tuple-element.59), channel_id=1, source_target_pairs={{0,16},{8,72},{16,32},{24,88},{32,48},{40,104},{48,0},{56,120},{64... | collective-permute-start | bytes 2359304 | tf_op jit(solution)/shard_map/ppermute | solution.py:46
  114.5 1.2 shard_map.105
  115.7 1.6 %collective-permute-start.34 = (bf16[8,128,384]{2,1,0:T(8,128)(2,1)S(1)}, bf16[8,128,384]{2,1,0:T(8,128)(2,1)S(1)}, u32[]{:S(2)}, u32[]{:S(2)}) collective-permute-start(bf16[8,128,384]{2,1,0:T(8,128)(2,1)S(1)} %get-tuple-element.60), channel_id=1, source_target_pairs={{0,48},{8,200},{16,0},{24,216},{32,16},{40,232},{48,32},{56,248},{... | collective-permute-start | bytes 2359304 | tf_op jit(solution)/shard_map/ppermute | solution.py:46
  117.4 3.2 %collective-permute-start.32 = (bf16[8,128,384]{2,1,0:T(8,128)(2,1)S(1)}, bf16[8,128,384]{2,1,0:T(8,128)(2,1)S(1)}, u32[]{:S(2)}, u32[]{:S(2)}) collective-permute-start(bf16[8,128,384]{2,1,0:T(8,128)(2,1)S(1)} %get-tuple-element.58), channel_id=1, source_target_pairs={{0,48},{8,200},{16,0},{24,216},{32,16},{40,232},{48,32},{56,248},{... | collective-permute-start | bytes 2359304 | tf_op jit(solution)/shard_map/ppermute | solution.py:46
  120.7 4.6 %collective-permute-done.21 = bf16[384,384]{1,0:T(8,128)(2,1)S(1)} collective-permute-done((bf16[384,384]{1,0:T(8,128)(2,1)S(1)}, bf16[384,384]{1,0:T(8,128)(2,1)S(1)}, u32[]{:S(2)}, u32[]{:S(2)}) %collective-permute-start.21) | collective-permute-done | bytes 294944 | tf_op jit(solution)/shard_map/ppermute | solution.py:420
  125.4 0.5 collective-permute-done.33.low_second
  125.9 1.6 %collective-permute-start.22 = (bf16[384,384]{1,0:T(8,128)(2,1)S(1)}, bf16[384,384]{1,0:T(8,128)(2,1)S(1)}, u32[]{:S(2)}, u32[]{:S(2)}) collective-permute-start(bf16[384,384]{1,0:T(8,128)(2,1)S(1)} %add_convert_fusion.4), channel_id=1, source_target_pairs={{0,1},{1,2},{2,3},{3,4},{4,5},{5,6},{6,7},{7,0},{8,9},{9,10},{10,1... | collective-permute-start | bytes 884744 | tf_op jit(solution)/shard_map/ppermute | solution.py:420
  127.5 0.5 collective-permute-done.34.high_second
  128.0 0.9 shard_map.108
  129.0 3.1 %collective-permute-done.26 = bf16[384,384]{1,0:T(8,128)(2,1)S(1)} collective-permute-done((bf16[384,384]{1,0:T(8,128)(2,1)S(1)}, bf16[384,384]{1,0:T(8,128)(2,1)S(1)}, u32[]{:S(2)}, u32[]{:S(2)}) %collective-permute-start.26) | collective-permute-done | bytes 294944 | tf_op jit(solution)/shard_map/ppermute | solution.py:420
  132.3 5.8 %collective-permute-done.32.high_first = bf16[8,128,384]{2,1,0:T(8,128)(2,1)S(1)} collective-permute-done((bf16[8,128,384]{2,1,0:T(8,128)(2,1)S(1)}, bf16[8,128,384]{2,1,0:T(8,128)(2,1)S(1)}, u32[]{:S(2)}, u32[]{:S(2)}) %collective-permute-start.32) | collective-permute-done | bytes 786464 | tf_op jit(solution)/shard_map/ppermute | solution.py:46
  138.0 1.3 shard_map.107
  139.6 3.2 %collective-permute-start.38 = (bf16[4,128,384]{2,1,0:T(8,128)(2,1)S(1)}, bf16[4,128,384]{2,1,0:T(8,128)(2,1)S(1)}, u32[]{:S(2)}, u32[]{:S(2)}) collective-permute-start(bf16[4,128,384]{2,1,0:T(8,128)(2,1)S(1)} %get-tuple-element.67), channel_id=1, source_target_pairs={{0,192},{8,56},{16,208},{24,8},{32,224},{40,24},{48,240},{56,40},{... | collective-permute-start | bytes 1179656 | tf_op jit(solution)/shard_map/ppermute | solution.py:46
  142.9 2.1 %collective-permute-start.23 = (bf16[384,384]{1,0:T(8,128)(2,1)S(1)}, bf16[384,384]{1,0:T(8,128)(2,1)S(1)}, u32[]{:S(2)}, u32[]{:S(2)}) collective-permute-start(bf16[384,384]{1,0:T(8,128)(2,1)S(1)} %add_convert_fusion.3), channel_id=1, source_target_pairs={{0,1},{1,2},{2,3},{3,4},{4,5},{5,6},{6,7},{7,0},{8,9},{9,10},{10,1... | collective-permute-start | bytes 884744 | tf_op jit(solution)/shard_map/ppermute | solution.py:420
  145.0 3.6 %collective-permute-done.37.from_low = bf16[4,128,384]{2,1,0:T(8,128)(2,1)S(1)} collective-permute-done((bf16[4,128,384]{2,1,0:T(8,128)(2,1)S(1)}, bf16[4,128,384]{2,1,0:T(8,128)(2,1)S(1)}, u32[]{:S(2)}, u32[]{:S(2)}) %collective-permute-start.37) | collective-permute-done | bytes 393248 | tf_op jit(solution)/shard_map/ppermute | solution.py:46
  148.8 2.6 %collective-permute-done.23 = bf16[384,384]{1,0:T(8,128)(2,1)S(1)} collective-permute-done((bf16[384,384]{1,0:T(8,128)(2,1)S(1)}, bf16[384,384]{1,0:T(8,128)(2,1)S(1)}, u32[]{:S(2)}, u32[]{:S(2)}) %collective-permute-start.23) | collective-permute-done | bytes 294944 | tf_op jit(solution)/shard_map/ppermute | solution.py:420
  151.3 0.8 add_convert_fusion
  152.2 1.6 %shard_map.111 = (bf16[384,384]{1,0:T(8,128)(2,1)}, bf16[384,384]{1,0:T(8,128)(2,1)}) custom-call(s32[96]{0:T(128)S(1)} %compare_select_fusion.1.refs_1_.refs_0_, s32[96]{0:T(128)S(1)} %convert_element_type.69.refs_1_, s32[1]{0:T(128)} %bitcast.2.refs_2_.refs_1_, f32[2,384,384]{2,1,0:T(8,128)S(1)} %get-tuple-element.52.refs_3_, ...), custom_call_target="tpu_custom_call" | custom-call | tf_op jit(solution)/shard_map/pallas_call | solution.py:438
  (93 shorter events, 2.8 us)
Async XLA Ops:
  0.6 0.7 copy-start.17
  2.5 1.5 collective-permute-start.8
  4.1 25.5 %copy-start.8 = (bf16[384,384]{1,0:T(8,128)(2,1)S(1)}, bf16[384,384]{1,0:T(8,128)(2,1)}, u32[]{:S(2)}) copy-start(bf16[384,384]{1,0:T(8,128)(2,1)} %refs_2_.4) | copy-start | bytes 884740
  4.1 41.2 %copy-start.18 = (s32[96,4]{0,1:T(4,128)S(1)}, s32[96,4]{0,1:T(4,128)}, u32[]{:S(2)}) copy-start(s32[96,4]{0,1:T(4,128)} %param.9) | copy-start | bytes 4612
  4.1 8.1 %collective-permute-start.13 = (bf16[4,128,384]{2,1,0:T(8,128)(2,1)S(1)}, bf16[4,128,384]{2,1,0:T(8,128)(2,1)S(1)}, u32[]{:S(2)}, u32[]{:S(2)}) collective-permute-start(bf16[4,128,384]{2,1,0:T(8,128)(2,1)S(1)} %shard_map.98.refs_0_), channel_id=1, source_target_pairs={{0,192},{8,56},{16,208},{24,8},{32,224},{40,24},{48,240},{56,40},{... | collective-permute-start | bytes 1179656 | tf_op jit(solution)/shard_map/ppermute | solution.py:46
  6.9 9.1 %collective-permute-start.9 = (bf16[4,128,384]{2,1,0:T(8,128)(2,1)S(1)}, bf16[4,128,384]{2,1,0:T(8,128)(2,1)S(1)}, u32[]{:S(2)}, u32[]{:S(2)}) collective-permute-start(bf16[4,128,384]{2,1,0:T(8,128)(2,1)S(1)} %shard_map.98.refs_0_), channel_id=1, source_target_pairs={{0,64},{8,24},{16,80},{24,40},{32,96},{40,56},{48,112},{56,8},{64,... | collective-permute-start | bytes 1179656 | tf_op jit(solution)/shard_map/ppermute | solution.py:46
  12.3 7.0 %collective-permute-start.15 = (bf16[2,128,384]{2,1,0:T(8,128)(2,1)S(1)}, bf16[2,128,384]{2,1,0:T(8,128)(2,1)S(1)}, u32[]{:S(2)}, u32[]{:S(2)}) collective-permute-start(bf16[2,128,384]{2,1,0:T(8,128)(2,1)S(1)} %slice.41), channel_id=1, source_target_pairs={{0,192},{8,56},{16,208},{24,8},{32,224},{40,24},{48,240},{56,40},{... | collective-permute-start | bytes 589832 | tf_op jit(solution)/shard_map/ppermute | solution.py:46
  16.1 9.1 %collective-permute-start.14 = (bf16[2,128,384]{2,1,0:T(8,128)(2,1)S(1)}, bf16[2,128,384]{2,1,0:T(8,128)(2,1)S(1)}, u32[]{:S(2)}, u32[]{:S(2)}) collective-permute-start(bf16[2,128,384]{2,1,0:T(8,128)(2,1)S(1)} %slice.40), channel_id=1, source_target_pairs={{0,64},{8,24},{16,80},{24,40},{32,96},{40,56},{48,112},{56,8},{64,... | collective-permute-start | bytes 589832 | tf_op jit(solution)/shard_map/ppermute | solution.py:46
  16.2 15.2 %collective-permute-start.10 = (bf16[8,128,384]{2,1,0:T(8,128)(2,1)S(1)}, bf16[8,128,384]{2,1,0:T(8,128)(2,1)}, u32[]{:S(2)}, u32[]{:S(2)}) collective-permute-start(bf16[8,128,384]{2,1,0:T(8,128)(2,1)S(1)} %shard_map.99.refs_1_.refs_7_), channel_id=1, source_target_pairs={{0,16},{8,72},{16,32},{24,88},{32,48},{40,104},{48,0},{56,120},{64... | collective-permute-start | bytes 2359304 | tf_op jit(solution)/shard_map/ppermute | solution.py:46
  26.1 12.3 %collective-permute-start.17 = (bf16[8,128,384]{2,1,0:T(8,128)(2,1)}, bf16[8,128,384]{2,1,0:T(8,128)(2,1)}, u32[]{:S(2)}, u32[]{:S(2)}) collective-permute-start(bf16[8,128,384]{2,1,0:T(8,128)(2,1)} %shard_map.100.refs_5_.refs_11_), channel_id=1, source_target_pairs={{0,48},{8,200},{16,0},{24,216},{32,16},{40,232},{48,32},{56,248},{... | collective-permute-start | bytes 2359304 | tf_op jit(solution)/shard_map/ppermute | solution.py:46
  26.5 23.7 %collective-permute-start.11 = (bf16[8,128,384]{2,1,0:T(8,128)(2,1)S(1)}, bf16[8,128,384]{2,1,0:T(8,128)(2,1)S(1)}, u32[]{:S(2)}, u32[]{:S(2)}) collective-permute-start(bf16[8,128,384]{2,1,0:T(8,128)(2,1)S(1)} %shard_map.99.refs_1_.refs_7_), channel_id=1, source_target_pairs={{0,48},{8,200},{16,0},{24,216},{32,16},{40,232},{48,32},{56,248},{... | collective-permute-start | bytes 2359304 | tf_op jit(solution)/shard_map/ppermute | solution.py:46
  29.5 10.6 %collective-permute-start = (bf16[384,384]{1,0:T(8,128)(2,1)S(1)}, bf16[384,384]{1,0:T(8,128)(2,1)S(1)}, u32[]{:S(2)}, u32[]{:S(2)}) collective-permute-start(bf16[384,384]{1,0:T(8,128)(2,1)S(1)} %copy-done.8), channel_id=1, source_target_pairs={{0,1},{1,2},{2,3},{3,4},{4,5},{5,6},{6,7},{7,0},{8,9},{9,10},{10,1... | collective-permute-start | bytes 884744 | tf_op jit(solution)/shard_map/ppermute | solution.py:420
  31.5 25.9 %collective-permute-start.16 = (bf16[8,128,384]{2,1,0:T(8,128)(2,1)}, bf16[8,128,384]{2,1,0:T(8,128)(2,1)}, u32[]{:S(2)}, u32[]{:S(2)}) collective-permute-start(bf16[8,128,384]{2,1,0:T(8,128)(2,1)} %shard_map.100.refs_5_.refs_11_), channel_id=1, source_target_pairs={{0,16},{8,72},{16,32},{24,88},{32,48},{40,104},{48,0},{56,120},{64... | collective-permute-start | bytes 2359304 | tf_op jit(solution)/shard_map/ppermute | solution.py:46
  31.5 25.9 %collective-permute-start.12 = (bf16[8,128,384]{2,1,0:T(8,128)(2,1)}, bf16[8,128,384]{2,1,0:T(8,128)(2,1)}, u32[]{:S(2)}, u32[]{:S(2)}) collective-permute-start(bf16[8,128,384]{2,1,0:T(8,128)(2,1)} %collective-permute-done.10.refs_2_.refs_8_), channel_id=1, source_target_pairs={{0,16},{8,72},{16,32},{24,88},{32,48},{40,104},{48,0},{56,120},{64... | collective-permute-start | bytes 2359304 | tf_op jit(solution)/shard_map/ppermute | solution.py:46
  38.4 19.0 %collective-permute-start.18 = (bf16[8,128,384]{2,1,0:T(8,128)(2,1)}, bf16[8,128,384]{2,1,0:T(8,128)(2,1)}, u32[]{:S(2)}, u32[]{:S(2)}) collective-permute-start(bf16[8,128,384]{2,1,0:T(8,128)(2,1)} %collective-permute-done.17.refs_7_.refs_13_), channel_id=1, source_target_pairs={{0,48},{8,200},{16,0},{24,216},{32,16},{40,232},{48,32},{56,248},{... | collective-permute-start | bytes 2359304 | tf_op jit(solution)/shard_map/ppermute | solution.py:46
  40.1 9.4 %collective-permute-start.1 = (bf16[384,384]{1,0:T(8,128)(2,1)S(1)}, bf16[384,384]{1,0:T(8,128)(2,1)}, u32[]{:S(2)}, u32[]{:S(2)}) collective-permute-start(bf16[384,384]{1,0:T(8,128)(2,1)S(1)} %copy-done.8), channel_id=1, source_target_pairs={{0,7},{1,0},{2,1},{3,2},{4,3},{5,4},{6,5},{7,6},{8,15},{9,8},{10,9... | collective-permute-start | bytes 884744 | tf_op jit(solution)/shard_map/ppermute | solution.py:420
  49.5 12.1 %collective-permute-start.2 = (bf16[384,384]{1,0:T(8,128)(2,1)S(1)}, bf16[384,384]{1,0:T(8,128)(2,1)S(1)}, u32[]{:S(2)}, u32[]{:S(2)}) collective-permute-start(bf16[384,384]{1,0:T(8,128)(2,1)S(1)} %collective-permute-done.refs_3_), channel_id=1, source_target_pairs={{0,1},{1,2},{2,3},{3,4},{4,5},{5,6},{6,7},{7,0},{8,9},{9,10},{10,1... | collective-permute-start | bytes 884744 | tf_op jit(solution)/shard_map/ppermute | solution.py:420
  49.5 0.7 copy-start.11
  50.2 0.9 copy-start.1
  51.1 10.6 %collective-permute-start.3 = (bf16[384,384]{1,0:T(8,128)(2,1)}, bf16[384,384]{1,0:T(8,128)(2,1)S(1)}, u32[]{:S(2)}, u32[]{:S(2)}) collective-permute-start(bf16[384,384]{1,0:T(8,128)(2,1)} %collective-permute-done.1.refs_4_), channel_id=1, source_target_pairs={{0,7},{1,0},{2,1},{3,2},{4,3},{5,4},{6,5},{7,6},{8,15},{9,8},{10,9... | collective-permute-start | bytes 884744 | tf_op jit(solution)/shard_map/ppermute | solution.py:420
  57.3 20.6 %copy-start = (bf16[384,3072]{1,0:T(8,128)(2,1)S(1)}, bf16[384,3072]{1,0:T(8,128)(2,1)}, u32[]{:S(2)}) copy-start(bf16[384,3072]{1,0:T(8,128)(2,1)} %refs_2_.7) | copy-start | bytes 7077892
  57.4 1.3 copy-start.2
  61.4 24.5 %collective-permute-start.19 = (bf16[6,128,384]{2,1,0:T(8,128)(2,1)}, bf16[6,128,384]{2,1,0:T(8,128)(2,1)}, u32[]{:S(2)}, u32[]{:S(2)}) collective-permute-start(bf16[6,128,384]{2,1,0:T(8,128)(2,1)} %shard_map.101), channel_id=1, source_target_pairs={{0,8},{8,0},{16,24},{24,16},{32,40},{40,32},{48,56},{56,48},{64,72... | collective-permute-start | bytes 1769480 | tf_op jit(solution)/shard_map/ppermute | solution.py:50
  61.6 12.4 %copy-start.13 = (bf16[384,384]{1,0:T(8,128)(2,1)}, bf16[384,384]{1,0:T(8,128)(2,1)S(1)}, u32[]{:S(2)}) copy-start(bf16[384,384]{1,0:T(8,128)(2,1)S(1)} %collective-permute-done.2.refs_5_) | copy-start | bytes 884740
  61.6 11.2 %collective-permute-start.4 = (bf16[384,384]{1,0:T(8,128)(2,1)S(1)}, bf16[384,384]{1,0:T(8,128)(2,1)S(1)}, u32[]{:S(2)}, u32[]{:S(2)}) collective-permute-start(bf16[384,384]{1,0:T(8,128)(2,1)S(1)} %collective-permute-done.2.refs_5_), channel_id=1, source_target_pairs={{0,1},{1,2},{2,3},{3,4},{4,5},{5,6},{6,7},{7,0},{8,9},{9,10},{10,1... | collective-permute-start | bytes 884744 | tf_op jit(solution)/shard_map/ppermute | solution.py:420
  61.7 13.0 %copy-start.15 = (bf16[384,384]{1,0:T(8,128)(2,1)}, bf16[384,384]{1,0:T(8,128)(2,1)S(1)}, u32[]{:S(2)}) copy-start(bf16[384,384]{1,0:T(8,128)(2,1)S(1)} %collective-permute-done.3.refs_6_) | copy-start | bytes 884740
  61.7 11.1 %collective-permute-start.5 = (bf16[384,384]{1,0:T(8,128)(2,1)S(1)}, bf16[384,384]{1,0:T(8,128)(2,1)S(1)}, u32[]{:S(2)}, u32[]{:S(2)}) collective-permute-start(bf16[384,384]{1,0:T(8,128)(2,1)S(1)} %collective-permute-done.3.refs_6_), channel_id=1, source_target_pairs={{0,7},{1,0},{2,1},{3,2},{4,3},{5,4},{6,5},{7,6},{8,15},{9,8},{10,9... | collective-permute-start | bytes 884744 | tf_op jit(solution)/shard_map/ppermute | solution.py:420
  73.9 0.7 copy-start.4
  74.6 9.4 %collective-permute-start.6 = (bf16[192,384]{1,0:T(8,128)(2,1)}, bf16[192,384]{1,0:T(8,128)(2,1)}, u32[]{:S(2)}, u32[]{:S(2)}) collective-permute-start(bf16[192,384]{1,0:T(8,128)(2,1)} %get-tuple-element.38), channel_id=1, source_target_pairs={{0,1},{1,2},{2,3},{3,4},{4,5},{5,6},{6,7},{7,0},{8,9},{9,10},{10,1... | collective-permute-start | bytes 442376 | tf_op jit(solution)/shard_map/ppermute | solution.py:420
  74.6 9.4 %collective-permute-start.7 = (bf16[192,384]{1,0:T(8,128)(2,1)}, bf16[192,384]{1,0:T(8,128)(2,1)}, u32[]{:S(2)}, u32[]{:S(2)}) collective-permute-start(bf16[192,384]{1,0:T(8,128)(2,1)} %get-tuple-element.39), channel_id=1, source_target_pairs={{0,7},{1,0},{2,1},{3,2},{4,3},{5,4},{6,5},{7,6},{8,15},{9,8},{10,9... | collective-permute-start | bytes 442376 | tf_op jit(solution)/shard_map/ppermute | solution.py:420
  77.9 6.2 %copy-start.5 = (bf16[384,384]{1,0:T(8,128)(2,1)S(1)}, bf16[384,384]{1,0:T(8,128)(2,1)}, u32[]{:S(2)}) copy-start(bf16[384,384]{1,0:T(8,128)(2,1)} %copy-done.4) | copy-start | bytes 884740
  77.9 1.0 copy-start.9
  78.9 1.0 copy-start.12
  79.8 1.0 copy-start.14
  80.8 1.0 copy-start.16
  84.0 1.9 %copy-start.3 = (bf16[8,128,384]{2,1,0:T(8,128)(2,1)S(1)}, bf16[8,128,384]{2,1,0:T(8,128)(2,1)}, u32[]{:S(2)}) copy-start(bf16[8,128,384]{2,1,0:T(8,128)(2,1)} %copy-done.1) | copy-start | bytes 2359300
  84.0 1.9 %copy-start.6 = (bf16[384,384]{1,0:T(8,128)(2,1)S(1)}, bf16[384,384]{1,0:T(8,128)(2,1)}, u32[]{:S(2)}) copy-start(bf16[384,384]{1,0:T(8,128)(2,1)} %refs_3_.3) | copy-start | bytes 884740
  84.0 1.9 %copy-start.7 = (bf16[384,384]{1,0:T(8,128)(2,1)S(1)}, bf16[384,384]{1,0:T(8,128)(2,1)}, u32[]{:S(2)}) copy-start(bf16[384,384]{1,0:T(8,128)(2,1)} %refs_4_.1) | copy-start | bytes 884740
  84.0 1.9 %copy-start.10 = (bf16[384,384]{1,0:T(8,128)(2,1)S(1)}, bf16[384,384]{1,0:T(8,128)(2,1)}, u32[]{:S(2)}) copy-start(bf16[384,384]{1,0:T(8,128)(2,1)} %refs_2_.6) | copy-start | bytes 884740
  93.8 2.1 %collective-permute-start.28 = (bf16[6,128,384]{2,1,0:T(8,128)(2,1)S(1)}, bf16[6,128,384]{2,1,0:T(8,128)(2,1)S(1)}, u32[]{:S(2)}, u32[]{:S(2)}) collective-permute-start(bf16[6,128,384]{2,1,0:T(8,128)(2,1)S(1)} %get-tuple-element.54), channel_id=1, source_target_pairs={{0,8},{8,0},{16,24},{24,16},{32,40},{40,32},{48,56},{56,48},{64,72... | collective-permute-start | bytes 1769480 | tf_op jit(solution)/shard_map/ppermute | solution.py:50
  97.0 17.5 %collective-permute-start.29 = (bf16[8,128,384]{2,1,0:T(8,128)(2,1)S(1)}, bf16[8,128,384]{2,1,0:T(8,128)(2,1)S(1)}, u32[]{:S(2)}, u32[]{:S(2)}) collective-permute-start(bf16[8,128,384]{2,1,0:T(8,128)(2,1)S(1)} %get-tuple-element.55), channel_id=1, source_target_pairs={{0,16},{8,72},{16,32},{24,88},{32,48},{40,104},{48,0},{56,120},{64... | collective-permute-start | bytes 2359304 | tf_op jit(solution)/shard_map/ppermute | solution.py:46
  99.2 15.3 %collective-permute-start.30 = (bf16[8,128,384]{2,1,0:T(8,128)(2,1)S(1)}, bf16[8,128,384]{2,1,0:T(8,128)(2,1)S(1)}, u32[]{:S(2)}, u32[]{:S(2)}) collective-permute-start(bf16[8,128,384]{2,1,0:T(8,128)(2,1)S(1)} %get-tuple-element.56), channel_id=1, source_target_pairs={{0,48},{8,200},{16,0},{24,216},{32,16},{40,232},{48,32},{56,248},{... | collective-permute-start | bytes 2359304 | tf_op jit(solution)/shard_map/ppermute | solution.py:46
  103.0 5.2 %collective-permute-start.24 = (bf16[192,384]{1,0:T(8,128)(2,1)S(1)}, bf16[192,384]{1,0:T(8,128)(2,1)S(1)}, u32[]{:S(2)}, u32[]{:S(2)}) collective-permute-start(bf16[192,384]{1,0:T(8,128)(2,1)S(1)} %get-tuple-element.73), channel_id=1, source_target_pairs={{0,7},{1,0},{2,1},{3,2},{4,3},{5,4},{6,5},{7,6},{8,15},{9,8},{10,9... | collective-permute-start | bytes 442376 | tf_op jit(solution)/shard_map/ppermute | solution.py:420
  104.8 12.4 %collective-permute-start.20 = (bf16[192,384]{1,0:T(8,128)(2,1)S(1)}, bf16[192,384]{1,0:T(8,128)(2,1)S(1)}, u32[]{:S(2)}, u32[]{:S(2)}) collective-permute-start(bf16[192,384]{1,0:T(8,128)(2,1)S(1)} %get-tuple-element.72), channel_id=1, source_target_pairs={{0,1},{1,2},{2,3},{3,4},{4,5},{5,6},{6,7},{7,0},{8,9},{9,10},{10,1... | collective-permute-start | bytes 442376 | tf_op jit(solution)/shard_map/ppermute | solution.py:420
  108.3 12.4 %collective-permute-start.25 = (bf16[384,384]{1,0:T(8,128)(2,1)S(1)}, bf16[384,384]{1,0:T(8,128)(2,1)S(1)}, u32[]{:S(2)}, u32[]{:S(2)}) collective-permute-start(bf16[384,384]{1,0:T(8,128)(2,1)S(1)} %pad_maximum_fusion.1), channel_id=1, source_target_pairs={{0,7},{1,0},{2,1},{3,2},{4,3},{5,4},{6,5},{7,6},{8,15},{9,8},{10,9... | collective-permute-start | bytes 884744 | tf_op jit(solution)/shard_map/ppermute | solution.py:420
  112.6 13.2 %collective-permute-start.33 = (bf16[8,128,384]{2,1,0:T(8,128)(2,1)S(1)}, bf16[8,128,384]{2,1,0:T(8,128)(2,1)S(1)}, u32[]{:S(2)}, u32[]{:S(2)}) collective-permute-start(bf16[8,128,384]{2,1,0:T(8,128)(2,1)S(1)} %get-tuple-element.59), channel_id=1, source_target_pairs={{0,16},{8,72},{16,32},{24,88},{32,48},{40,104},{48,0},{56,120},{64... | collective-permute-start | bytes 2359304 | tf_op jit(solution)/shard_map/ppermute | solution.py:46
  115.7 12.3 %collective-permute-start.34 = (bf16[8,128,384]{2,1,0:T(8,128)(2,1)S(1)}, bf16[8,128,384]{2,1,0:T(8,128)(2,1)S(1)}, u32[]{:S(2)}, u32[]{:S(2)}) collective-permute-start(bf16[8,128,384]{2,1,0:T(8,128)(2,1)S(1)} %get-tuple-element.60), channel_id=1, source_target_pairs={{0,48},{8,200},{16,0},{24,216},{32,16},{40,232},{48,32},{56,248},{... | collective-permute-start | bytes 2359304 | tf_op jit(solution)/shard_map/ppermute | solution.py:46
  117.3 8.0 %collective-permute-start.21 = (bf16[384,384]{1,0:T(8,128)(2,1)S(1)}, bf16[384,384]{1,0:T(8,128)(2,1)S(1)}, u32[]{:S(2)}, u32[]{:S(2)}) collective-permute-start(bf16[384,384]{1,0:T(8,128)(2,1)S(1)} %pad_maximum_fusion), channel_id=1, source_target_pairs={{0,1},{1,2},{2,3},{3,4},{4,5},{5,6},{6,7},{7,0},{8,9},{9,10},{10,1... | collective-permute-start | bytes 884744 | tf_op jit(solution)/shard_map/ppermute | solution.py:420
  117.4 20.6 %collective-permute-start.32 = (bf16[8,128,384]{2,1,0:T(8,128)(2,1)S(1)}, bf16[8,128,384]{2,1,0:T(8,128)(2,1)S(1)}, u32[]{:S(2)}, u32[]{:S(2)}) collective-permute-start(bf16[8,128,384]{2,1,0:T(8,128)(2,1)S(1)} %get-tuple-element.58), channel_id=1, source_target_pairs={{0,48},{8,200},{16,0},{24,216},{32,16},{40,232},{48,32},{56,248},{... | collective-permute-start | bytes 2359304 | tf_op jit(solution)/shard_map/ppermute | solution.py:46
  120.6 17.4 %collective-permute-start.31 = (bf16[8,128,384]{2,1,0:T(8,128)(2,1)S(1)}, bf16[8,128,384]{2,1,0:T(8,128)(2,1)S(1)}, u32[]{:S(2)}, u32[]{:S(2)}) collective-permute-start(bf16[8,128,384]{2,1,0:T(8,128)(2,1)S(1)} %get-tuple-element.57), channel_id=1, source_target_pairs={{0,16},{8,72},{16,32},{24,88},{32,48},{40,104},{48,0},{56,120},{64... | collective-permute-start | bytes 2359304 | tf_op jit(solution)/shard_map/ppermute | solution.py:46
  125.3 6.7 %collective-permute-start.26 = (bf16[384,384]{1,0:T(8,128)(2,1)S(1)}, bf16[384,384]{1,0:T(8,128)(2,1)S(1)}, u32[]{:S(2)}, u32[]{:S(2)}) collective-permute-start(bf16[384,384]{1,0:T(8,128)(2,1)S(1)} %add_convert_fusion.2), channel_id=1, source_target_pairs={{0,7},{1,0},{2,1},{3,2},{4,3},{5,4},{6,5},{7,6},{8,15},{9,8},{10,9... | collective-permute-start | bytes 884744 | tf_op jit(solution)/shard_map/ppermute | solution.py:420
  125.9 16.9 %collective-permute-start.22 = (bf16[384,384]{1,0:T(8,128)(2,1)S(1)}, bf16[384,384]{1,0:T(8,128)(2,1)S(1)}, u32[]{:S(2)}, u32[]{:S(2)}) collective-permute-start(bf16[384,384]{1,0:T(8,128)(2,1)S(1)} %add_convert_fusion.4), channel_id=1, source_target_pairs={{0,1},{1,2},{2,3},{3,4},{4,5},{5,6},{6,7},{7,0},{8,9},{9,10},{10,1... | collective-permute-start | bytes 884744 | tf_op jit(solution)/shard_map/ppermute | solution.py:420
  128.9 10.5 %collective-permute-start.35 = (bf16[2,128,384]{2,1,0:T(8,128)(2,1)S(1)}, bf16[2,128,384]{2,1,0:T(8,128)(2,1)S(1)}, u32[]{:S(2)}, u32[]{:S(2)}) collective-permute-start(bf16[2,128,384]{2,1,0:T(8,128)(2,1)S(1)} %get-tuple-element.64), channel_id=1, source_target_pairs={{0,64},{8,24},{16,80},{24,40},{32,96},{40,56},{48,112},{56,8},{64,... | collective-permute-start | bytes 589832 | tf_op jit(solution)/shard_map/ppermute | solution.py:46
  132.0 7.3 %collective-permute-start.36 = (bf16[2,128,384]{2,1,0:T(8,128)(2,1)S(1)}, bf16[2,128,384]{2,1,0:T(8,128)(2,1)S(1)}, u32[]{:S(2)}, u32[]{:S(2)}) collective-permute-start(bf16[2,128,384]{2,1,0:T(8,128)(2,1)S(1)} %get-tuple-element.65), channel_id=1, source_target_pairs={{0,192},{8,56},{16,208},{24,8},{32,224},{40,24},{48,240},{56,40},{... | collective-permute-start | bytes 589832 | tf_op jit(solution)/shard_map/ppermute | solution.py:46
  138.0 10.8 %collective-permute-start.27 = (bf16[384,384]{1,0:T(8,128)(2,1)S(1)}, bf16[384,384]{1,0:T(8,128)(2,1)S(1)}, u32[]{:S(2)}, u32[]{:S(2)}) collective-permute-start(bf16[384,384]{1,0:T(8,128)(2,1)S(1)} %add_convert_fusion.1), channel_id=1, source_target_pairs={{0,7},{1,0},{2,1},{3,2},{4,3},{5,4},{6,5},{7,6},{8,15},{9,8},{10,9... | collective-permute-start | bytes 884744 | tf_op jit(solution)/shard_map/ppermute | solution.py:420
  139.5 9.1 %collective-permute-start.37 = (bf16[4,128,384]{2,1,0:T(8,128)(2,1)S(1)}, bf16[4,128,384]{2,1,0:T(8,128)(2,1)S(1)}, u32[]{:S(2)}, u32[]{:S(2)}) collective-permute-start(bf16[4,128,384]{2,1,0:T(8,128)(2,1)S(1)} %get-tuple-element.66), channel_id=1, source_target_pairs={{0,64},{8,24},{16,80},{24,40},{32,96},{40,56},{48,112},{56,8},{64,... | collective-permute-start | bytes 1179656 | tf_op jit(solution)/shard_map/ppermute | solution.py:46
  139.6 9.0 %collective-permute-start.38 = (bf16[4,128,384]{2,1,0:T(8,128)(2,1)S(1)}, bf16[4,128,384]{2,1,0:T(8,128)(2,1)S(1)}, u32[]{:S(2)}, u32[]{:S(2)}) collective-permute-start(bf16[4,128,384]{2,1,0:T(8,128)(2,1)S(1)} %get-tuple-element.67), channel_id=1, source_target_pairs={{0,192},{8,56},{16,208},{24,8},{32,224},{40,24},{48,240},{56,40},{... | collective-permute-start | bytes 1179656 | tf_op jit(solution)/shard_map/ppermute | solution.py:46
  142.9 8.5 %collective-permute-start.23 = (bf16[384,384]{1,0:T(8,128)(2,1)S(1)}, bf16[384,384]{1,0:T(8,128)(2,1)S(1)}, u32[]{:S(2)}, u32[]{:S(2)}) collective-permute-start(bf16[384,384]{1,0:T(8,128)(2,1)S(1)} %add_convert_fusion.3), channel_id=1, source_target_pairs={{0,1},{1,2},{2,3},{3,4},{4,5},{5,6},{6,7},{7,0},{8,9},{9,10},{10,1... | collective-permute-start | bytes 884744 | tf_op jit(solution)/shard_map/ppermute | solution.py:420
  148.7 3.5 %collective-permute-start.39 = (bf16[2,128,384]{2,1,0:T(8,128)(2,1)S(1)}, bf16[2,128,384]{2,1,0:T(8,128)(2,1)S(1)}, u32[]{:S(2)}, u32[]{:S(2)}) collective-permute-start(bf16[2,128,384]{2,1,0:T(8,128)(2,1)S(1)} %get-tuple-element.69), channel_id=1, source_target_pairs={{0,8},{8,0},{16,24},{24,16},{32,40},{40,32},{48,56},{56,48},{64,72... | collective-permute-start | bytes 589832 | tf_op jit(solution)/shard_map/ppermute | solution.py:50

commit v2 on v1

--- a/solution.py
+++ b/solution.py
@@ -62,11 +62,15 @@
 
 
 def fetch(gathered, code, target, sem):
-    for kind, source in enumerate(gathered):
-
-        @pl.when(code // 16 == kind)
+    for first in range(0, len(gathered), 4):
+
+        @pl.when((code >= first * 16) & (code < (first + 4) * 16))
         def _():
-            pltpu.make_async_copy(source.at[code % 16], target, sem).start()
+            for kind in range(first, first + 4):
+
+                @pl.when((code >= kind * 16) & (code < (kind + 1) * 16))
+                def _():
+                    pltpu.make_async_copy(gathered[kind].at[code - kind * 16], target, sem).start()
 
 
 def join_body(*refs):

time: 156 us -> 156 us (level)
  no operation moved by 1% of the time
where the time goes in v2:
time: 156 us; the launch traced here: 154 us
  waiting for transfers between devices  57.2 us (37%)
  starting transfers between devices  55.4 us (36%)
  Pallas kernels  29.7 us (19%)
  local copies, waits for them, and re-layouts  8.52 us (5%)
    pallas_call x19, Pallas kernels, call(): pl.pallas_call(body, in_specs=in_specs, out_specs=out_specs or [VMEM] * l...  29.7 us
    ppermute x20, waiting for transfers between devices, hop(): return lax.ppermute(x, 'seq', steps_of(leg, sign))  28.5 us
    ppermute x20, starting transfers between devices, hop(): return lax.ppermute(x, 'seq', steps_of(leg, sign))  27.4 us
    ppermute x16, starting transfers between devices, ring_pair(): lax.ppermute(x, 'head', [(i, (i + sign) % size) for i in range(size)])  27.1 us
    ppermute x16, waiting for transfers between devices, ring_pair(): lax.ppermute(x, 'head', [(i, (i + sign) % size) for i in range(size)])  25.3 us
    unnamed x39, local copies, waits for them, and re-layouts  8.31 us
    ppermute x4, waiting for transfers between devices, swap(): return lax.ppermute(x, 'seq', swap_of())  3.42 us
  transfers between devices with their start and end apart: 40, of which 17 were waited for; matrix products, arithmetic and copies ran while one was open for 1% of the time, Pallas kernels for 12%

profile of v2, /device:TPU:8, one launch (start us, length us, event | category | flops | bytes accessed | tf_op | source)
XLA Modules:
  0.0 153.5 jit_solution(5727096802411397838)
XLA Ops:
  0.6 0.7 copy-done.17
  1.3 1.2 shard_map.97
  2.6 1.4 collective-permute-done.8.refs_1_
  4.1 2.8 %collective-permute-start.13 = (bf16[4,128,384]{2,1,0:T(8,128)(2,1)S(1)}, bf16[4,128,384]{2,1,0:T(8,128)(2,1)S(1)}, u32[]{:S(2)}, u32[]{:S(2)}) collective-permute-start(bf16[4,128,384]{2,1,0:T(8,128)(2,1)S(1)} %shard_map.98.refs_0_), channel_id=1, source_target_pairs={{0,192},{8,56},{16,208},{24,8},{32,224},{40,24},{48,240},{56,40},{... | collective-permute-start | bytes 1179656 | tf_op jit(solution)/shard_map/ppermute | solution.py:46
  6.9 5.3 %collective-permute-done.13.refs_0_ = bf16[4,128,384]{2,1,0:T(8,128)(2,1)S(1)} collective-permute-done((bf16[4,128,384]{2,1,0:T(8,128)(2,1)S(1)}, bf16[4,128,384]{2,1,0:T(8,128)(2,1)S(1)}, u32[]{:S(2)}, u32[]{:S(2)}) %collective-permute-start.13) | collective-permute-done | bytes 393248 | tf_op jit(solution)/shard_map/ppermute | solution.py:46
  12.3 3.8 %collective-permute-start.15 = (bf16[2,128,384]{2,1,0:T(8,128)(2,1)S(1)}, bf16[2,128,384]{2,1,0:T(8,128)(2,1)S(1)}, u32[]{:S(2)}, u32[]{:S(2)}) collective-permute-start(bf16[2,128,384]{2,1,0:T(8,128)(2,1)S(1)} %slice.41), channel_id=1, source_target_pairs={{0,192},{8,56},{16,208},{24,8},{32,224},{40,24},{48,240},{56,40},{... | collective-permute-start | bytes 589832 | tf_op jit(solution)/shard_map/ppermute | solution.py:46
  16.2 1.7 %collective-permute-start.10 = (bf16[8,128,384]{2,1,0:T(8,128)(2,1)S(1)}, bf16[8,128,384]{2,1,0:T(8,128)(2,1)}, u32[]{:S(2)}, u32[]{:S(2)}) collective-permute-start(bf16[8,128,384]{2,1,0:T(8,128)(2,1)S(1)} %shard_map.99.refs_1_.refs_7_), channel_id=1, source_target_pairs={{0,16},{8,72},{16,32},{24,88},{32,48},{40,104},{48,0},{56,120},{64... | collective-permute-start | bytes 2359304 | tf_op jit(solution)/shard_map/ppermute | solution.py:46
  17.9 1.3 collective-permute-done.15.refs_2_
  19.2 5.9 %collective-permute-done.14.refs_1_ = bf16[2,128,384]{2,1,0:T(8,128)(2,1)S(1)} collective-permute-done((bf16[2,128,384]{2,1,0:T(8,128)(2,1)S(1)}, bf16[2,128,384]{2,1,0:T(8,128)(2,1)S(1)}, u32[]{:S(2)}, u32[]{:S(2)}) %collective-permute-start.14) | collective-permute-done | bytes 196640 | tf_op jit(solution)/shard_map/ppermute | solution.py:46
  25.1 1.0 shard_map.100.refs_5_.refs_11_
  26.1 0.5 collective-permute-start.17
  26.5 3.0 %collective-permute-start.11 = (bf16[8,128,384]{2,1,0:T(8,128)(2,1)S(1)}, bf16[8,128,384]{2,1,0:T(8,128)(2,1)S(1)}, u32[]{:S(2)}, u32[]{:S(2)}) collective-permute-start(bf16[8,128,384]{2,1,0:T(8,128)(2,1)S(1)} %shard_map.99.refs_1_.refs_7_), channel_id=1, source_target_pairs={{0,48},{8,200},{16,0},{24,216},{32,16},{40,232},{48,32},{56,248},{... | collective-permute-start | bytes 2359304 | tf_op jit(solution)/shard_map/ppermute | solution.py:46
  29.5 1.9 %collective-permute-start = (bf16[384,384]{1,0:T(8,128)(2,1)S(1)}, bf16[384,384]{1,0:T(8,128)(2,1)S(1)}, u32[]{:S(2)}, u32[]{:S(2)}) collective-permute-start(bf16[384,384]{1,0:T(8,128)(2,1)S(1)} %copy-done.8), channel_id=1, source_target_pairs={{0,1},{1,2},{2,3},{3,4},{4,5},{5,6},{6,7},{7,0},{8,9},{9,10},{10,1... | collective-permute-start | bytes 884744 | tf_op jit(solution)/shard_map/ppermute | solution.py:424
  31.5 0.6 collective-permute-start.12
  32.0 6.3 %collective-permute-done.17.refs_7_.refs_13_ = bf16[8,128,384]{2,1,0:T(8,128)(2,1)} collective-permute-done((bf16[8,128,384]{2,1,0:T(8,128)(2,1)}, bf16[8,128,384]{2,1,0:T(8,128)(2,1)}, u32[]{:S(2)}, u32[]{:S(2)}) %collective-permute-start.17) | collective-permute-done | bytes 786464 | tf_op jit(solution)/shard_map/ppermute | solution.py:46
  38.4 1.0 collective-permute-start.18
  39.4 0.7 collective-permute-done.refs_3_
  40.1 5.1 %collective-permute-start.1 = (bf16[384,384]{1,0:T(8,128)(2,1)S(1)}, bf16[384,384]{1,0:T(8,128)(2,1)}, u32[]{:S(2)}, u32[]{:S(2)}) collective-permute-start(bf16[384,384]{1,0:T(8,128)(2,1)S(1)} %copy-done.8), channel_id=1, source_target_pairs={{0,7},{1,0},{2,1},{3,2},{4,3},{5,4},{6,5},{7,6},{8,15},{9,8},{10,9... | collective-permute-start | bytes 884744 | tf_op jit(solution)/shard_map/ppermute | solution.py:424
  45.5 4.0 %collective-permute-done.1.refs_4_ = bf16[384,384]{1,0:T(8,128)(2,1)} collective-permute-done((bf16[384,384]{1,0:T(8,128)(2,1)S(1)}, bf16[384,384]{1,0:T(8,128)(2,1)}, u32[]{:S(2)}, u32[]{:S(2)}) %collective-permute-start.1) | collective-permute-done | bytes 294944 | tf_op jit(solution)/shard_map/ppermute | solution.py:424
  49.5 0.7 copy-done.11
  50.2 0.9 copy-done.1
  51.1 3.9 %collective-permute-start.3 = (bf16[384,384]{1,0:T(8,128)(2,1)}, bf16[384,384]{1,0:T(8,128)(2,1)S(1)}, u32[]{:S(2)}, u32[]{:S(2)}) collective-permute-start(bf16[384,384]{1,0:T(8,128)(2,1)} %collective-permute-done.1.refs_4_), channel_id=1, source_target_pairs={{0,7},{1,0},{2,1},{3,2},{4,3},{5,4},{6,5},{7,6},{8,15},{9,8},{10,9... | collective-permute-start | bytes 884744 | tf_op jit(solution)/shard_map/ppermute | solution.py:424
  55.1 2.2 %shard_map.93.refs_0_.table = s32[49]{0:T(128)S(1)} custom-call(s32[4,96]{1,0:T(4,128)S(1)} %bitcast.6, s32[96]{0:T(128)S(1)} %compare_select_fusion.1.refs_1_.refs_0_, s32[1]{0:T(128)} %bitcast.2.refs_2_.refs_1_), custom_call_target="tpu_custom_call" | custom-call | tf_op jit(solution)/shard_map/pallas_call | solution.py:442
  57.4 1.3 copy-done.2
  58.7 2.8 %shard_map.101 = bf16[6,128,384]{2,1,0:T(8,128)(2,1)} custom-call(s32[49]{0:T(128)S(1)} %shard_map.93.refs_0_.table, bf16[8,128,384]{2,1,0:T(8,128)(2,1)S(1)} %shard_map.99.refs_1_.refs_7_, bf16[8,128,384]{2,1,0:T(8,128)(2,1)} %collective-permute-done.10.refs_2_.refs_8_, bf16[8,128,384]{2,1,0:T(8,128)(2,1)S(1)} %copy-done.2, ...), custom_call_target="tpu_custom_call" | custom-call | tf_op jit(solution)/shard_map/pallas_call | solution.py:442
  61.7 3.6 %collective-permute-start.5 = (bf16[384,384]{1,0:T(8,128)(2,1)S(1)}, bf16[384,384]{1,0:T(8,128)(2,1)S(1)}, u32[]{:S(2)}, u32[]{:S(2)}) collective-permute-start(bf16[384,384]{1,0:T(8,128)(2,1)S(1)} %collective-permute-done.3.refs_6_), channel_id=1, source_target_pairs={{0,7},{1,0},{2,1},{3,2},{4,3},{5,4},{6,5},{7,6},{8,15},{9,8},{10,9... | collective-permute-start | bytes 884744 | tf_op jit(solution)/shard_map/ppermute | solution.py:424
  65.3 7.5 %collective-permute-done.4.low.refs_3_ = bf16[384,384]{1,0:T(8,128)(2,1)S(1)} collective-permute-done((bf16[384,384]{1,0:T(8,128)(2,1)S(1)}, bf16[384,384]{1,0:T(8,128)(2,1)S(1)}, u32[]{:S(2)}, u32[]{:S(2)}) %collective-permute-start.4) | collective-permute-done | bytes 294944 | tf_op jit(solution)/shard_map/ppermute | solution.py:424
  72.8 1.1 shard_map.95
  73.9 0.7 copy-done.4
  74.7 3.2 %collective-permute-start.7 = (bf16[192,384]{1,0:T(8,128)(2,1)}, bf16[192,384]{1,0:T(8,128)(2,1)}, u32[]{:S(2)}, u32[]{:S(2)}) collective-permute-start(bf16[192,384]{1,0:T(8,128)(2,1)} %get-tuple-element.39), channel_id=1, source_target_pairs={{0,7},{1,0},{2,1},{3,2},{4,3},{5,4},{6,5},{7,6},{8,15},{9,8},{10,9... | collective-permute-start | bytes 442376 | tf_op jit(solution)/shard_map/ppermute | solution.py:424
  77.9 1.0 copy-done.9
  78.9 1.0 copy-done.12
  79.9 1.0 copy-done.14
  80.8 1.0 copy-done.16
  81.8 2.2 %shard_map.94.refs_2_ = f32[384,384]{1,0:T(8,128)S(1)} custom-call(s32[1]{0:T(128)} %bitcast.refs_0_, bf16[384,3072]{1,0:T(8,128)(2,1)S(1)} %copy-done, bf16[384,384]{1,0:T(8,128)(2,1)S(1)} %copy-done.9, bf16[384,384]{1,0:T(8,128)(2,1)S(1)} %copy-done.12, bf16[384,384]{1,0:T(8,128)(2,1)} %collective-permute-done.1.refs_4_, bf16[384,384]{1,0:T(8,128)(2,1)S(1)} %copy-done.14, ...), custom_call_target="tpu_custom_call" | custom-call | tf_op jit(solution)/shard_map/pallas_call | solution.py:442
  84.1 1.8 %shard_map.96.refs_5_ = bf16[384,384]{1,0:T(8,128)(2,1)S(1)} custom-call(s32[1]{0:T(128)} %bitcast.refs_0_, bf16[384,3072]{1,0:T(8,128)(2,1)S(1)} %copy-done, f32[384,384]{1,0:T(8,128)S(1)} %shard_map.94.refs_2_, bf16[384,384]{1,0:T(8,128)(2,1)S(1)} %collective-permute-done.4.low.refs_3_, bf16[384,384]{1,0:T(8,128)(2,1)S(1)} %copy-done.5, ...), custom_call_target="tpu_custom_call" | custom-call | tf_op jit(solution)/shard_map/pallas_call | solution.py:442
  86.0 7.9 %shard_map.102 = (bf16[384,384]{1,0:T(8,128)(2,1)S(1)}, bf16[384,384]{1,0:T(8,128)(2,1)}, f32[2,384,384]{2,1,0:T(8,128)S(1)}, bf16[6,128,384]{2,1,0:T(8,128)(2,1)S(1)}, bf16[6,128,384]{2,1,0:T(8,128)(2,1)S(1)}) custom-call(s32[49]{0:T(128)S(1)} %shard_map.93.refs_0_.table, s32[1]{0:T(128)} %bitcast.2.refs_2_.refs_1_, bf16[384,384]{1,0:T(8,128)(2,1)S(1)} %copy-done.10, ...), custom_call_target="tpu_custom_call" | custom-call | tf_op jit(solution)/shard_map/pallas_call | solution.py:442
  94.0 2.0 %collective-permute-done.28.refs_2_.theirs = bf16[6,128,384]{2,1,0:T(8,128)(2,1)S(1)} collective-permute-done((bf16[6,128,384]{2,1,0:T(8,128)(2,1)S(1)}, bf16[6,128,384]{2,1,0:T(8,128)(2,1)S(1)}, u32[]{:S(2)}, u32[]{:S(2)}) %collective-permute-start.28) | collective-permute-done | bytes 589856 | tf_op jit(solution)/shard_map/ppermute | solution.py:50
  96.0 1.1 shard_map.104
  97.0 2.2 %collective-permute-start.29 = (bf16[8,128,384]{2,1,0:T(8,128)(2,1)S(1)}, bf16[8,128,384]{2,1,0:T(8,128)(2,1)S(1)}, u32[]{:S(2)}, u32[]{:S(2)}) collective-permute-start(bf16[8,128,384]{2,1,0:T(8,128)(2,1)S(1)} %get-tuple-element.55), channel_id=1, source_target_pairs={{0,16},{8,72},{16,32},{24,88},{32,48},{40,104},{48,0},{56,120},{64... | collective-permute-start | bytes 2359304 | tf_op jit(solution)/shard_map/ppermute | solution.py:46
  99.2 1.7 %collective-permute-start.30 = (bf16[8,128,384]{2,1,0:T(8,128)(2,1)S(1)}, bf16[8,128,384]{2,1,0:T(8,128)(2,1)S(1)}, u32[]{:S(2)}, u32[]{:S(2)}) collective-permute-start(bf16[8,128,384]{2,1,0:T(8,128)(2,1)S(1)} %get-tuple-element.56), channel_id=1, source_target_pairs={{0,48},{8,200},{16,0},{24,216},{32,16},{40,232},{48,32},{56,248},{... | collective-permute-start | bytes 2359304 | tf_op jit(solution)/shard_map/ppermute | solution.py:46
  100.9 2.1 %shard_map.103 = (bf16[384,384]{1,0:T(8,128)(2,1)S(1)}, bf16[384,384]{1,0:T(8,128)(2,1)S(1)}, bf16[384,384]{1,0:T(8,128)(2,1)S(1)}, bf16[384,384]{1,0:T(8,128)(2...) custom-call(s32[1]{0:T(128)} %bitcast.refs_0_, ...), custom_call_target="tpu_custom_call" | custom-call | tf_op jit(solution)/shard_map/pallas_call | solution.py:442
  103.0 1.8 %collective-permute-start.24 = (bf16[192,384]{1,0:T(8,128)(2,1)S(1)}, bf16[192,384]{1,0:T(8,128)(2,1)S(1)}, u32[]{:S(2)}, u32[]{:S(2)}) collective-permute-start(bf16[192,384]{1,0:T(8,128)(2,1)S(1)} %get-tuple-element.73), channel_id=1, source_target_pairs={{0,7},{1,0},{2,1},{3,2},{4,3},{5,4},{6,5},{7,6},{8,15},{9,8},{10,9... | collective-permute-start | bytes 442376 | tf_op jit(solution)/shard_map/ppermute | solution.py:424
  105.2 3.0 %collective-permute-done.24 = bf16[192,384]{1,0:T(8,128)(2,1)S(1)} collective-permute-done((bf16[192,384]{1,0:T(8,128)(2,1)S(1)}, bf16[192,384]{1,0:T(8,128)(2,1)S(1)}, u32[]{:S(2)}, u32[]{:S(2)}) %collective-permute-start.24) | collective-permute-done | bytes 147488 | tf_op jit(solution)/shard_map/ppermute | solution.py:424
  108.3 3.3 %collective-permute-start.25 = (bf16[384,384]{1,0:T(8,128)(2,1)S(1)}, bf16[384,384]{1,0:T(8,128)(2,1)S(1)}, u32[]{:S(2)}, u32[]{:S(2)}) collective-permute-start(bf16[384,384]{1,0:T(8,128)(2,1)S(1)} %pad_maximum_fusion.1), channel_id=1, source_target_pairs={{0,7},{1,0},{2,1},{3,2},{4,3},{5,4},{6,5},{7,6},{8,15},{9,8},{10,9... | collective-permute-start | bytes 884744 | tf_op jit(solution)/shard_map/ppermute | solution.py:424
  111.6 1.1 shard_map.106
  112.7 1.8 %collective-permute-start.33 = (bf16[8,128,384]{2,1,0:T(8,128)(2,1)S(1)}, bf16[8,128,384]{2,1,0:T(8,128)(2,1)S(1)}, u32[]{:S(2)}, u32[]{:S(2)}) collective-permute-start(bf16[8,128,384]{2,1,0:T(8,128)(2,1)S(1)} %get-tuple-element.59), channel_id=1, source_target_pairs={{0,16},{8,72},{16,32},{24,88},{32,48},{40,104},{48,0},{56,120},{64... | collective-permute-start | bytes 2359304 | tf_op jit(solution)/shard_map/ppermute | solution.py:46
  114.6 1.2 shard_map.105
  115.7 1.5 %collective-permute-start.34 = (bf16[8,128,384]{2,1,0:T(8,128)(2,1)S(1)}, bf16[8,128,384]{2,1,0:T(8,128)(2,1)S(1)}, u32[]{:S(2)}, u32[]{:S(2)}) collective-permute-start(bf16[8,128,384]{2,1,0:T(8,128)(2,1)S(1)} %get-tuple-element.60), channel_id=1, source_target_pairs={{0,48},{8,200},{16,0},{24,216},{32,16},{40,232},{48,32},{56,248},{... | collective-permute-start | bytes 2359304 | tf_op jit(solution)/shard_map/ppermute | solution.py:46
  117.5 3.2 %collective-permute-start.32 = (bf16[8,128,384]{2,1,0:T(8,128)(2,1)S(1)}, bf16[8,128,384]{2,1,0:T(8,128)(2,1)S(1)}, u32[]{:S(2)}, u32[]{:S(2)}) collective-permute-start(bf16[8,128,384]{2,1,0:T(8,128)(2,1)S(1)} %get-tuple-element.58), channel_id=1, source_target_pairs={{0,48},{8,200},{16,0},{24,216},{32,16},{40,232},{48,32},{56,248},{... | collective-permute-start | bytes 2359304 | tf_op jit(solution)/shard_map/ppermute | solution.py:46
  120.8 4.6 %collective-permute-done.21 = bf16[384,384]{1,0:T(8,128)(2,1)S(1)} collective-permute-done((bf16[384,384]{1,0:T(8,128)(2,1)S(1)}, bf16[384,384]{1,0:T(8,128)(2,1)S(1)}, u32[]{:S(2)}, u32[]{:S(2)}) %collective-permute-start.21) | collective-permute-done | bytes 294944 | tf_op jit(solution)/shard_map/ppermute | solution.py:424
  125.5 0.5 collective-permute-done.33.low_second
  126.0 1.6 %collective-permute-start.22 = (bf16[384,384]{1,0:T(8,128)(2,1)S(1)}, bf16[384,384]{1,0:T(8,128)(2,1)S(1)}, u32[]{:S(2)}, u32[]{:S(2)}) collective-permute-start(bf16[384,384]{1,0:T(8,128)(2,1)S(1)} %add_convert_fusion.4), channel_id=1, source_target_pairs={{0,1},{1,2},{2,3},{3,4},{4,5},{5,6},{6,7},{7,0},{8,9},{9,10},{10,1... | collective-permute-start | bytes 884744 | tf_op jit(solution)/shard_map/ppermute | solution.py:424
  127.9 0.9 shard_map.108
  129.0 3.1 %collective-permute-done.26 = bf16[384,384]{1,0:T(8,128)(2,1)S(1)} collective-permute-done((bf16[384,384]{1,0:T(8,128)(2,1)S(1)}, bf16[384,384]{1,0:T(8,128)(2,1)S(1)}, u32[]{:S(2)}, u32[]{:S(2)}) %collective-permute-start.26) | collective-permute-done | bytes 294944 | tf_op jit(solution)/shard_map/ppermute | solution.py:424
  132.3 5.2 %collective-permute-done.32.high_first = bf16[8,128,384]{2,1,0:T(8,128)(2,1)S(1)} collective-permute-done((bf16[8,128,384]{2,1,0:T(8,128)(2,1)S(1)}, bf16[8,128,384]{2,1,0:T(8,128)(2,1)S(1)}, u32[]{:S(2)}, u32[]{:S(2)}) %collective-permute-start.32) | collective-permute-done | bytes 786464 | tf_op jit(solution)/shard_map/ppermute | solution.py:46
  137.5 1.3 shard_map.107
  139.0 3.2 %collective-permute-start.38 = (bf16[4,128,384]{2,1,0:T(8,128)(2,1)S(1)}, bf16[4,128,384]{2,1,0:T(8,128)(2,1)S(1)}, u32[]{:S(2)}, u32[]{:S(2)}) collective-permute-start(bf16[4,128,384]{2,1,0:T(8,128)(2,1)S(1)} %get-tuple-element.67), channel_id=1, source_target_pairs={{0,192},{8,56},{16,208},{24,8},{32,224},{40,24},{48,240},{56,40},{... | collective-permute-start | bytes 1179656 | tf_op jit(solution)/shard_map/ppermute | solution.py:46
  142.3 2.1 %collective-permute-start.23 = (bf16[384,384]{1,0:T(8,128)(2,1)S(1)}, bf16[384,384]{1,0:T(8,128)(2,1)S(1)}, u32[]{:S(2)}, u32[]{:S(2)}) collective-permute-start(bf16[384,384]{1,0:T(8,128)(2,1)S(1)} %add_convert_fusion.3), channel_id=1, source_target_pairs={{0,1},{1,2},{2,3},{3,4},{4,5},{5,6},{6,7},{7,0},{8,9},{9,10},{10,1... | collective-permute-start | bytes 884744 | tf_op jit(solution)/shard_map/ppermute | solution.py:424
  144.4 3.6 %collective-permute-done.37.from_low = bf16[4,128,384]{2,1,0:T(8,128)(2,1)S(1)} collective-permute-done((bf16[4,128,384]{2,1,0:T(8,128)(2,1)S(1)}, bf16[4,128,384]{2,1,0:T(8,128)(2,1)S(1)}, u32[]{:S(2)}, u32[]{:S(2)}) %collective-permute-start.37) | collective-permute-done | bytes 393248 | tf_op jit(solution)/shard_map/ppermute | solution.py:46
  148.1 0.6 collective-permute-start.39
  148.7 2.4 %collective-permute-done.23 = bf16[384,384]{1,0:T(8,128)(2,1)S(1)} collective-permute-done((bf16[384,384]{1,0:T(8,128)(2,1)S(1)}, bf16[384,384]{1,0:T(8,128)(2,1)S(1)}, u32[]{:S(2)}, u32[]{:S(2)}) %collective-permute-start.23) | collective-permute-done | bytes 294944 | tf_op jit(solution)/shard_map/ppermute | solution.py:424
  151.1 0.8 add_convert_fusion
  151.9 1.6 %shard_map.111 = (bf16[384,384]{1,0:T(8,128)(2,1)}, bf16[384,384]{1,0:T(8,128)(2,1)}) custom-call(s32[96]{0:T(128)S(1)} %compare_select_fusion.1.refs_1_.refs_0_, s32[96]{0:T(128)S(1)} %convert_element_type.69.refs_1_, s32[1]{0:T(128)} %bitcast.2.refs_2_.refs_1_, f32[2,384,384]{2,1,0:T(8,128)S(1)} %get-tuple-element.52.refs_3_, ...), custom_call_target="tpu_custom_call" | custom-call | tf_op jit(solution)/shard_map/pallas_call | solution.py:442
  (93 shorter events, 3.0 us)
Async XLA Ops:
  0.6 0.7 copy-start.17
  2.5 1.5 collective-permute-start.8
  4.1 25.5 %copy-start.8 = (bf16[384,384]{1,0:T(8,128)(2,1)S(1)}, bf16[384,384]{1,0:T(8,128)(2,1)}, u32[]{:S(2)}) copy-start(bf16[384,384]{1,0:T(8,128)(2,1)} %refs_2_.4) | copy-start | bytes 884740
  4.1 41.2 %copy-start.18 = (s32[96,4]{0,1:T(4,128)S(1)}, s32[96,4]{0,1:T(4,128)}, u32[]{:S(2)}) copy-start(s32[96,4]{0,1:T(4,128)} %param.9) | copy-start | bytes 4612
  4.1 8.1 %collective-permute-start.13 = (bf16[4,128,384]{2,1,0:T(8,128)(2,1)S(1)}, bf16[4,128,384]{2,1,0:T(8,128)(2,1)S(1)}, u32[]{:S(2)}, u32[]{:S(2)}) collective-permute-start(bf16[4,128,384]{2,1,0:T(8,128)(2,1)S(1)} %shard_map.98.refs_0_), channel_id=1, source_target_pairs={{0,192},{8,56},{16,208},{24,8},{32,224},{40,24},{48,240},{56,40},{... | collective-permute-start | bytes 1179656 | tf_op jit(solution)/shard_map/ppermute | solution.py:46
  6.9 9.1 %collective-permute-start.9 = (bf16[4,128,384]{2,1,0:T(8,128)(2,1)S(1)}, bf16[4,128,384]{2,1,0:T(8,128)(2,1)S(1)}, u32[]{:S(2)}, u32[]{:S(2)}) collective-permute-start(bf16[4,128,384]{2,1,0:T(8,128)(2,1)S(1)} %shard_map.98.refs_0_), channel_id=1, source_target_pairs={{0,64},{8,24},{16,80},{24,40},{32,96},{40,56},{48,112},{56,8},{64,... | collective-permute-start | bytes 1179656 | tf_op jit(solution)/shard_map/ppermute | solution.py:46
  12.3 7.0 %collective-permute-start.15 = (bf16[2,128,384]{2,1,0:T(8,128)(2,1)S(1)}, bf16[2,128,384]{2,1,0:T(8,128)(2,1)S(1)}, u32[]{:S(2)}, u32[]{:S(2)}) collective-permute-start(bf16[2,128,384]{2,1,0:T(8,128)(2,1)S(1)} %slice.41), channel_id=1, source_target_pairs={{0,192},{8,56},{16,208},{24,8},{32,224},{40,24},{48,240},{56,40},{... | collective-permute-start | bytes 589832 | tf_op jit(solution)/shard_map/ppermute | solution.py:46
  16.1 9.1 %collective-permute-start.14 = (bf16[2,128,384]{2,1,0:T(8,128)(2,1)S(1)}, bf16[2,128,384]{2,1,0:T(8,128)(2,1)S(1)}, u32[]{:S(2)}, u32[]{:S(2)}) collective-permute-start(bf16[2,128,384]{2,1,0:T(8,128)(2,1)S(1)} %slice.40), channel_id=1, source_target_pairs={{0,64},{8,24},{16,80},{24,40},{32,96},{40,56},{48,112},{56,8},{64,... | collective-permute-start | bytes 589832 | tf_op jit(solution)/shard_map/ppermute | solution.py:46
  16.2 15.2 %collective-permute-start.10 = (bf16[8,128,384]{2,1,0:T(8,128)(2,1)S(1)}, bf16[8,128,384]{2,1,0:T(8,128)(2,1)}, u32[]{:S(2)}, u32[]{:S(2)}) collective-permute-start(bf16[8,128,384]{2,1,0:T(8,128)(2,1)S(1)} %shard_map.99.refs_1_.refs_7_), channel_id=1, source_target_pairs={{0,16},{8,72},{16,32},{24,88},{32,48},{40,104},{48,0},{56,120},{64... | collective-permute-start | bytes 2359304 | tf_op jit(solution)/shard_map/ppermute | solution.py:46
  26.1 12.3 %collective-permute-start.17 = (bf16[8,128,384]{2,1,0:T(8,128)(2,1)}, bf16[8,128,384]{2,1,0:T(8,128)(2,1)}, u32[]{:S(2)}, u32[]{:S(2)}) collective-permute-start(bf16[8,128,384]{2,1,0:T(8,128)(2,1)} %shard_map.100.refs_5_.refs_11_), channel_id=1, source_target_pairs={{0,48},{8,200},{16,0},{24,216},{32,16},{40,232},{48,32},{56,248},{... | collective-permute-start | bytes 2359304 | tf_op jit(solution)/shard_map/ppermute | solution.py:46
  26.5 23.7 %collective-permute-start.11 = (bf16[8,128,384]{2,1,0:T(8,128)(2,1)S(1)}, bf16[8,128,384]{2,1,0:T(8,128)(2,1)S(1)}, u32[]{:S(2)}, u32[]{:S(2)}) collective-permute-start(bf16[8,128,384]{2,1,0:T(8,128)(2,1)S(1)} %shard_map.99.refs_1_.refs_7_), channel_id=1, source_target_pairs={{0,48},{8,200},{16,0},{24,216},{32,16},{40,232},{48,32},{56,248},{... | collective-permute-start | bytes 2359304 | tf_op jit(solution)/shard_map/ppermute | solution.py:46
  29.5 10.6 %collective-permute-start = (bf16[384,384]{1,0:T(8,128)(2,1)S(1)}, bf16[384,384]{1,0:T(8,128)(2,1)S(1)}, u32[]{:S(2)}, u32[]{:S(2)}) collective-permute-start(bf16[384,384]{1,0:T(8,128)(2,1)S(1)} %copy-done.8), channel_id=1, source_target_pairs={{0,1},{1,2},{2,3},{3,4},{4,5},{5,6},{6,7},{7,0},{8,9},{9,10},{10,1... | collective-permute-start | bytes 884744 | tf_op jit(solution)/shard_map/ppermute | solution.py:424
  31.5 25.9 %collective-permute-start.16 = (bf16[8,128,384]{2,1,0:T(8,128)(2,1)}, bf16[8,128,384]{2,1,0:T(8,128)(2,1)}, u32[]{:S(2)}, u32[]{:S(2)}) collective-permute-start(bf16[8,128,384]{2,1,0:T(8,128)(2,1)} %shard_map.100.refs_5_.refs_11_), channel_id=1, source_target_pairs={{0,16},{8,72},{16,32},{24,88},{32,48},{40,104},{48,0},{56,120},{64... | collective-permute-start | bytes 2359304 | tf_op jit(solution)/shard_map/ppermute | solution.py:46
  31.5 25.9 %collective-permute-start.12 = (bf16[8,128,384]{2,1,0:T(8,128)(2,1)}, bf16[8,128,384]{2,1,0:T(8,128)(2,1)}, u32[]{:S(2)}, u32[]{:S(2)}) collective-permute-start(bf16[8,128,384]{2,1,0:T(8,128)(2,1)} %collective-permute-done.10.refs_2_.refs_8_), channel_id=1, source_target_pairs={{0,16},{8,72},{16,32},{24,88},{32,48},{40,104},{48,0},{56,120},{64... | collective-permute-start | bytes 2359304 | tf_op jit(solution)/shard_map/ppermute | solution.py:46
  38.4 19.0 %collective-permute-start.18 = (bf16[8,128,384]{2,1,0:T(8,128)(2,1)}, bf16[8,128,384]{2,1,0:T(8,128)(2,1)}, u32[]{:S(2)}, u32[]{:S(2)}) collective-permute-start(bf16[8,128,384]{2,1,0:T(8,128)(2,1)} %collective-permute-done.17.refs_7_.refs_13_), channel_id=1, source_target_pairs={{0,48},{8,200},{16,0},{24,216},{32,16},{40,232},{48,32},{56,248},{... | collective-permute-start | bytes 2359304 | tf_op jit(solution)/shard_map/ppermute | solution.py:46
  40.1 9.4 %collective-permute-start.1 = (bf16[384,384]{1,0:T(8,128)(2,1)S(1)}, bf16[384,384]{1,0:T(8,128)(2,1)}, u32[]{:S(2)}, u32[]{:S(2)}) collective-permute-start(bf16[384,384]{1,0:T(8,128)(2,1)S(1)} %copy-done.8), channel_id=1, source_target_pairs={{0,7},{1,0},{2,1},{3,2},{4,3},{5,4},{6,5},{7,6},{8,15},{9,8},{10,9... | collective-permute-start | bytes 884744 | tf_op jit(solution)/shard_map/ppermute | solution.py:424
  49.5 12.1 %collective-permute-start.2 = (bf16[384,384]{1,0:T(8,128)(2,1)S(1)}, bf16[384,384]{1,0:T(8,128)(2,1)S(1)}, u32[]{:S(2)}, u32[]{:S(2)}) collective-permute-start(bf16[384,384]{1,0:T(8,128)(2,1)S(1)} %collective-permute-done.refs_3_), channel_id=1, source_target_pairs={{0,1},{1,2},{2,3},{3,4},{4,5},{5,6},{6,7},{7,0},{8,9},{9,10},{10,1... | collective-permute-start | bytes 884744 | tf_op jit(solution)/shard_map/ppermute | solution.py:424
  49.5 0.7 copy-start.11
  50.2 0.9 copy-start.1
  51.1 10.6 %collective-permute-start.3 = (bf16[384,384]{1,0:T(8,128)(2,1)}, bf16[384,384]{1,0:T(8,128)(2,1)S(1)}, u32[]{:S(2)}, u32[]{:S(2)}) collective-permute-start(bf16[384,384]{1,0:T(8,128)(2,1)} %collective-permute-done.1.refs_4_), channel_id=1, source_target_pairs={{0,7},{1,0},{2,1},{3,2},{4,3},{5,4},{6,5},{7,6},{8,15},{9,8},{10,9... | collective-permute-start | bytes 884744 | tf_op jit(solution)/shard_map/ppermute | solution.py:424
  57.3 20.6 %copy-start = (bf16[384,3072]{1,0:T(8,128)(2,1)S(1)}, bf16[384,3072]{1,0:T(8,128)(2,1)}, u32[]{:S(2)}) copy-start(bf16[384,3072]{1,0:T(8,128)(2,1)} %refs_2_.7) | copy-start | bytes 7077892
  57.4 1.3 copy-start.2
  61.5 24.5 %collective-permute-start.19 = (bf16[6,128,384]{2,1,0:T(8,128)(2,1)}, bf16[6,128,384]{2,1,0:T(8,128)(2,1)}, u32[]{:S(2)}, u32[]{:S(2)}) collective-permute-start(bf16[6,128,384]{2,1,0:T(8,128)(2,1)} %shard_map.101), channel_id=1, source_target_pairs={{0,8},{8,0},{16,24},{24,16},{32,40},{40,32},{48,56},{56,48},{64,72... | collective-permute-start | bytes 1769480 | tf_op jit(solution)/shard_map/ppermute | solution.py:50
  61.6 12.4 %copy-start.13 = (bf16[384,384]{1,0:T(8,128)(2,1)}, bf16[384,384]{1,0:T(8,128)(2,1)S(1)}, u32[]{:S(2)}) copy-start(bf16[384,384]{1,0:T(8,128)(2,1)S(1)} %collective-permute-done.2.refs_5_) | copy-start | bytes 884740
  61.6 11.2 %collective-permute-start.4 = (bf16[384,384]{1,0:T(8,128)(2,1)S(1)}, bf16[384,384]{1,0:T(8,128)(2,1)S(1)}, u32[]{:S(2)}, u32[]{:S(2)}) collective-permute-start(bf16[384,384]{1,0:T(8,128)(2,1)S(1)} %collective-permute-done.2.refs_5_), channel_id=1, source_target_pairs={{0,1},{1,2},{2,3},{3,4},{4,5},{5,6},{6,7},{7,0},{8,9},{9,10},{10,1... | collective-permute-start | bytes 884744 | tf_op jit(solution)/shard_map/ppermute | solution.py:424
  61.7 13.0 %copy-start.15 = (bf16[384,384]{1,0:T(8,128)(2,1)}, bf16[384,384]{1,0:T(8,128)(2,1)S(1)}, u32[]{:S(2)}) copy-start(bf16[384,384]{1,0:T(8,128)(2,1)S(1)} %collective-permute-done.3.refs_6_) | copy-start | bytes 884740
  61.7 11.1 %collective-permute-start.5 = (bf16[384,384]{1,0:T(8,128)(2,1)S(1)}, bf16[384,384]{1,0:T(8,128)(2,1)S(1)}, u32[]{:S(2)}, u32[]{:S(2)}) collective-permute-start(bf16[384,384]{1,0:T(8,128)(2,1)S(1)} %collective-permute-done.3.refs_6_), channel_id=1, source_target_pairs={{0,7},{1,0},{2,1},{3,2},{4,3},{5,4},{6,5},{7,6},{8,15},{9,8},{10,9... | collective-permute-start | bytes 884744 | tf_op jit(solution)/shard_map/ppermute | solution.py:424
  73.9 0.7 copy-start.4
  74.6 9.4 %collective-permute-start.6 = (bf16[192,384]{1,0:T(8,128)(2,1)}, bf16[192,384]{1,0:T(8,128)(2,1)}, u32[]{:S(2)}, u32[]{:S(2)}) collective-permute-start(bf16[192,384]{1,0:T(8,128)(2,1)} %get-tuple-element.38), channel_id=1, source_target_pairs={{0,1},{1,2},{2,3},{3,4},{4,5},{5,6},{6,7},{7,0},{8,9},{9,10},{10,1... | collective-permute-start | bytes 442376 | tf_op jit(solution)/shard_map/ppermute | solution.py:424
  74.7 9.4 %collective-permute-start.7 = (bf16[192,384]{1,0:T(8,128)(2,1)}, bf16[192,384]{1,0:T(8,128)(2,1)}, u32[]{:S(2)}, u32[]{:S(2)}) collective-permute-start(bf16[192,384]{1,0:T(8,128)(2,1)} %get-tuple-element.39), channel_id=1, source_target_pairs={{0,7},{1,0},{2,1},{3,2},{4,3},{5,4},{6,5},{7,6},{8,15},{9,8},{10,9... | collective-permute-start | bytes 442376 | tf_op jit(solution)/shard_map/ppermute | solution.py:424
  77.9 6.2 %copy-start.5 = (bf16[384,384]{1,0:T(8,128)(2,1)S(1)}, bf16[384,384]{1,0:T(8,128)(2,1)}, u32[]{:S(2)}) copy-start(bf16[384,384]{1,0:T(8,128)(2,1)} %copy-done.4) | copy-start | bytes 884740
  77.9 1.0 copy-start.9
  78.9 1.0 copy-start.12
  79.9 1.0 copy-start.14
  80.8 1.0 copy-start.16
  84.0 1.9 %copy-start.3 = (bf16[8,128,384]{2,1,0:T(8,128)(2,1)S(1)}, bf16[8,128,384]{2,1,0:T(8,128)(2,1)}, u32[]{:S(2)}) copy-start(bf16[8,128,384]{2,1,0:T(8,128)(2,1)} %copy-done.1) | copy-start | bytes 2359300
  84.0 1.9 %copy-start.6 = (bf16[384,384]{1,0:T(8,128)(2,1)S(1)}, bf16[384,384]{1,0:T(8,128)(2,1)}, u32[]{:S(2)}) copy-start(bf16[384,384]{1,0:T(8,128)(2,1)} %refs_3_.3) | copy-start | bytes 884740
  84.0 1.9 %copy-start.7 = (bf16[384,384]{1,0:T(8,128)(2,1)S(1)}, bf16[384,384]{1,0:T(8,128)(2,1)}, u32[]{:S(2)}) copy-start(bf16[384,384]{1,0:T(8,128)(2,1)} %refs_4_.1) | copy-start | bytes 884740
  84.0 1.9 %copy-start.10 = (bf16[384,384]{1,0:T(8,128)(2,1)S(1)}, bf16[384,384]{1,0:T(8,128)(2,1)}, u32[]{:S(2)}) copy-start(bf16[384,384]{1,0:T(8,128)(2,1)} %refs_2_.6) | copy-start | bytes 884740
  93.9 2.1 %collective-permute-start.28 = (bf16[6,128,384]{2,1,0:T(8,128)(2,1)S(1)}, bf16[6,128,384]{2,1,0:T(8,128)(2,1)S(1)}, u32[]{:S(2)}, u32[]{:S(2)}) collective-permute-start(bf16[6,128,384]{2,1,0:T(8,128)(2,1)S(1)} %get-tuple-element.54), channel_id=1, source_target_pairs={{0,8},{8,0},{16,24},{24,16},{32,40},{40,32},{48,56},{56,48},{64,72... | collective-permute-start | bytes 1769480 | tf_op jit(solution)/shard_map/ppermute | solution.py:50
  97.0 17.5 %collective-permute-start.29 = (bf16[8,128,384]{2,1,0:T(8,128)(2,1)S(1)}, bf16[8,128,384]{2,1,0:T(8,128)(2,1)S(1)}, u32[]{:S(2)}, u32[]{:S(2)}) collective-permute-start(bf16[8,128,384]{2,1,0:T(8,128)(2,1)S(1)} %get-tuple-element.55), channel_id=1, source_target_pairs={{0,16},{8,72},{16,32},{24,88},{32,48},{40,104},{48,0},{56,120},{64... | collective-permute-start | bytes 2359304 | tf_op jit(solution)/shard_map/ppermute | solution.py:46
  99.2 15.3 %collective-permute-start.30 = (bf16[8,128,384]{2,1,0:T(8,128)(2,1)S(1)}, bf16[8,128,384]{2,1,0:T(8,128)(2,1)S(1)}, u32[]{:S(2)}, u32[]{:S(2)}) collective-permute-start(bf16[8,128,384]{2,1,0:T(8,128)(2,1)S(1)} %get-tuple-element.56), channel_id=1, source_target_pairs={{0,48},{8,200},{16,0},{24,216},{32,16},{40,232},{48,32},{56,248},{... | collective-permute-start | bytes 2359304 | tf_op jit(solution)/shard_map/ppermute | solution.py:46
  103.0 5.2 %collective-permute-start.24 = (bf16[192,384]{1,0:T(8,128)(2,1)S(1)}, bf16[192,384]{1,0:T(8,128)(2,1)S(1)}, u32[]{:S(2)}, u32[]{:S(2)}) collective-permute-start(bf16[192,384]{1,0:T(8,128)(2,1)S(1)} %get-tuple-element.73), channel_id=1, source_target_pairs={{0,7},{1,0},{2,1},{3,2},{4,3},{5,4},{6,5},{7,6},{8,15},{9,8},{10,9... | collective-permute-start | bytes 442376 | tf_op jit(solution)/shard_map/ppermute | solution.py:424
  104.9 12.4 %collective-permute-start.20 = (bf16[192,384]{1,0:T(8,128)(2,1)S(1)}, bf16[192,384]{1,0:T(8,128)(2,1)S(1)}, u32[]{:S(2)}, u32[]{:S(2)}) collective-permute-start(bf16[192,384]{1,0:T(8,128)(2,1)S(1)} %get-tuple-element.72), channel_id=1, source_target_pairs={{0,1},{1,2},{2,3},{3,4},{4,5},{5,6},{6,7},{7,0},{8,9},{9,10},{10,1... | collective-permute-start | bytes 442376 | tf_op jit(solution)/shard_map/ppermute | solution.py:424
  108.3 12.4 %collective-permute-start.25 = (bf16[384,384]{1,0:T(8,128)(2,1)S(1)}, bf16[384,384]{1,0:T(8,128)(2,1)S(1)}, u32[]{:S(2)}, u32[]{:S(2)}) collective-permute-start(bf16[384,384]{1,0:T(8,128)(2,1)S(1)} %pad_maximum_fusion.1), channel_id=1, source_target_pairs={{0,7},{1,0},{2,1},{3,2},{4,3},{5,4},{6,5},{7,6},{8,15},{9,8},{10,9... | collective-permute-start | bytes 884744 | tf_op jit(solution)/shard_map/ppermute | solution.py:424
  112.7 13.2 %collective-permute-start.33 = (bf16[8,128,384]{2,1,0:T(8,128)(2,1)S(1)}, bf16[8,128,384]{2,1,0:T(8,128)(2,1)S(1)}, u32[]{:S(2)}, u32[]{:S(2)}) collective-permute-start(bf16[8,128,384]{2,1,0:T(8,128)(2,1)S(1)} %get-tuple-element.59), channel_id=1, source_target_pairs={{0,16},{8,72},{16,32},{24,88},{32,48},{40,104},{48,0},{56,120},{64... | collective-permute-start | bytes 2359304 | tf_op jit(solution)/shard_map/ppermute | solution.py:46
  115.7 12.2 %collective-permute-start.34 = (bf16[8,128,384]{2,1,0:T(8,128)(2,1)S(1)}, bf16[8,128,384]{2,1,0:T(8,128)(2,1)S(1)}, u32[]{:S(2)}, u32[]{:S(2)}) collective-permute-start(bf16[8,128,384]{2,1,0:T(8,128)(2,1)S(1)} %get-tuple-element.60), channel_id=1, source_target_pairs={{0,48},{8,200},{16,0},{24,216},{32,16},{40,232},{48,32},{56,248},{... | collective-permute-start | bytes 2359304 | tf_op jit(solution)/shard_map/ppermute | solution.py:46
  117.4 8.0 %collective-permute-start.21 = (bf16[384,384]{1,0:T(8,128)(2,1)S(1)}, bf16[384,384]{1,0:T(8,128)(2,1)S(1)}, u32[]{:S(2)}, u32[]{:S(2)}) collective-permute-start(bf16[384,384]{1,0:T(8,128)(2,1)S(1)} %pad_maximum_fusion), channel_id=1, source_target_pairs={{0,1},{1,2},{2,3},{3,4},{4,5},{5,6},{6,7},{7,0},{8,9},{9,10},{10,1... | collective-permute-start | bytes 884744 | tf_op jit(solution)/shard_map/ppermute | solution.py:424
  117.5 20.0 %collective-permute-start.32 = (bf16[8,128,384]{2,1,0:T(8,128)(2,1)S(1)}, bf16[8,128,384]{2,1,0:T(8,128)(2,1)S(1)}, u32[]{:S(2)}, u32[]{:S(2)}) collective-permute-start(bf16[8,128,384]{2,1,0:T(8,128)(2,1)S(1)} %get-tuple-element.58), channel_id=1, source_target_pairs={{0,48},{8,200},{16,0},{24,216},{32,16},{40,232},{48,32},{56,248},{... | collective-permute-start | bytes 2359304 | tf_op jit(solution)/shard_map/ppermute | solution.py:46
  120.7 16.8 %collective-permute-start.31 = (bf16[8,128,384]{2,1,0:T(8,128)(2,1)S(1)}, bf16[8,128,384]{2,1,0:T(8,128)(2,1)S(1)}, u32[]{:S(2)}, u32[]{:S(2)}) collective-permute-start(bf16[8,128,384]{2,1,0:T(8,128)(2,1)S(1)} %get-tuple-element.57), channel_id=1, source_target_pairs={{0,16},{8,72},{16,32},{24,88},{32,48},{40,104},{48,0},{56,120},{64... | collective-permute-start | bytes 2359304 | tf_op jit(solution)/shard_map/ppermute | solution.py:46
  125.4 6.7 %collective-permute-start.26 = (bf16[384,384]{1,0:T(8,128)(2,1)S(1)}, bf16[384,384]{1,0:T(8,128)(2,1)S(1)}, u32[]{:S(2)}, u32[]{:S(2)}) collective-permute-start(bf16[384,384]{1,0:T(8,128)(2,1)S(1)} %add_convert_fusion.2), channel_id=1, source_target_pairs={{0,7},{1,0},{2,1},{3,2},{4,3},{5,4},{6,5},{7,6},{8,15},{9,8},{10,9... | collective-permute-start | bytes 884744 | tf_op jit(solution)/shard_map/ppermute | solution.py:424
  126.0 16.3 %collective-permute-start.22 = (bf16[384,384]{1,0:T(8,128)(2,1)S(1)}, bf16[384,384]{1,0:T(8,128)(2,1)S(1)}, u32[]{:S(2)}, u32[]{:S(2)}) collective-permute-start(bf16[384,384]{1,0:T(8,128)(2,1)S(1)} %add_convert_fusion.4), channel_id=1, source_target_pairs={{0,1},{1,2},{2,3},{3,4},{4,5},{5,6},{6,7},{7,0},{8,9},{9,10},{10,1... | collective-permute-start | bytes 884744 | tf_op jit(solution)/shard_map/ppermute | solution.py:424
  128.9 9.9 %collective-permute-start.35 = (bf16[2,128,384]{2,1,0:T(8,128)(2,1)S(1)}, bf16[2,128,384]{2,1,0:T(8,128)(2,1)S(1)}, u32[]{:S(2)}, u32[]{:S(2)}) collective-permute-start(bf16[2,128,384]{2,1,0:T(8,128)(2,1)S(1)} %get-tuple-element.64), channel_id=1, source_target_pairs={{0,64},{8,24},{16,80},{24,40},{32,96},{40,56},{48,112},{56,8},{64,... | collective-permute-start | bytes 589832 | tf_op jit(solution)/shard_map/ppermute | solution.py:46
  132.1 6.7 %collective-permute-start.36 = (bf16[2,128,384]{2,1,0:T(8,128)(2,1)S(1)}, bf16[2,128,384]{2,1,0:T(8,128)(2,1)S(1)}, u32[]{:S(2)}, u32[]{:S(2)}) collective-permute-start(bf16[2,128,384]{2,1,0:T(8,128)(2,1)S(1)} %get-tuple-element.65), channel_id=1, source_target_pairs={{0,192},{8,56},{16,208},{24,8},{32,224},{40,24},{48,240},{56,40},{... | collective-permute-start | bytes 589832 | tf_op jit(solution)/shard_map/ppermute | solution.py:46
  137.5 11.3 %collective-permute-start.27 = (bf16[384,384]{1,0:T(8,128)(2,1)S(1)}, bf16[384,384]{1,0:T(8,128)(2,1)S(1)}, u32[]{:S(2)}, u32[]{:S(2)}) collective-permute-start(bf16[384,384]{1,0:T(8,128)(2,1)S(1)} %add_convert_fusion.1), channel_id=1, source_target_pairs={{0,7},{1,0},{2,1},{3,2},{4,3},{5,4},{6,5},{7,6},{8,15},{9,8},{10,9... | collective-permute-start | bytes 884744 | tf_op jit(solution)/shard_map/ppermute | solution.py:424
  138.9 9.1 %collective-permute-start.37 = (bf16[4,128,384]{2,1,0:T(8,128)(2,1)S(1)}, bf16[4,128,384]{2,1,0:T(8,128)(2,1)S(1)}, u32[]{:S(2)}, u32[]{:S(2)}) collective-permute-start(bf16[4,128,384]{2,1,0:T(8,128)(2,1)S(1)} %get-tuple-element.66), channel_id=1, source_target_pairs={{0,64},{8,24},{16,80},{24,40},{32,96},{40,56},{48,112},{56,8},{64,... | collective-permute-start | bytes 1179656 | tf_op jit(solution)/shard_map/ppermute | solution.py:46
  139.0 9.0 %collective-permute-start.38 = (bf16[4,128,384]{2,1,0:T(8,128)(2,1)S(1)}, bf16[4,128,384]{2,1,0:T(8,128)(2,1)S(1)}, u32[]{:S(2)}, u32[]{:S(2)}) collective-permute-start(bf16[4,128,384]{2,1,0:T(8,128)(2,1)S(1)} %get-tuple-element.67), channel_id=1, source_target_pairs={{0,192},{8,56},{16,208},{24,8},{32,224},{40,24},{48,240},{56,40},{... | collective-permute-start | bytes 1179656 | tf_op jit(solution)/shard_map/ppermute | solution.py:46
  142.3 8.8 %collective-permute-start.23 = (bf16[384,384]{1,0:T(8,128)(2,1)S(1)}, bf16[384,384]{1,0:T(8,128)(2,1)S(1)}, u32[]{:S(2)}, u32[]{:S(2)}) collective-permute-start(bf16[384,384]{1,0:T(8,128)(2,1)S(1)} %add_convert_fusion.3), channel_id=1, source_target_pairs={{0,1},{1,2},{2,3},{3,4},{4,5},{5,6},{6,7},{7,0},{8,9},{9,10},{10,1... | collective-permute-start | bytes 884744 | tf_op jit(solution)/shard_map/ppermute | solution.py:424
  148.1 3.8 %collective-permute-start.39 = (bf16[2,128,384]{2,1,0:T(8,128)(2,1)S(1)}, bf16[2,128,384]{2,1,0:T(8,128)(2,1)S(1)}, u32[]{:S(2)}, u32[]{:S(2)}) collective-permute-start(bf16[2,128,384]{2,1,0:T(8,128)(2,1)S(1)} %get-tuple-element.69), channel_id=1, source_target_pairs={{0,8},{8,0},{16,24},{24,16},{32,40},{40,32},{48,56},{56,48},{64,72... | collective-permute-start | bytes 589832 | tf_op jit(solution)/shard_map/ppermute | solution.py:50
